TPU v7x, 128 devices: a whole 4x4x4 slice. The times are simulated.
128 devices in a mesh: row: 4 (over x), col: 8 (over z_lo, y), layer: 4 (over z_hi, core).
Axes of the slice: x: 4, y: 4, z: 4 (z_hi: 2, z_lo: 2; z = z_hi * 2 + z_lo), core: 2. Of those that a mesh axis runs over, the one named last changes fastest.
Arguments:
- a_blocks: float32 [4096, 4096], P('row', ('col', 'layer')), may hold values from -6 to 6
- mask_a: int32 [64, 64], P('row', ('col', 'layer')), may hold values from 0 to 1, as said below
- b_blocks: float32 [4096, 32768], P('row', ('col', 'layer')), may hold values from -0.25 to 0.25
- mask_b: int32 [64, 512], P('row', ('col', 'layer')), may hold values from 0 to 1
Outputs:
- product: float32 [4096, 32768], P('row', ('col', 'layer'))
Inputs may be any that keep to these rules, and one draw needn't show every extreme that they name: Within one device's shard of mask_a (16 block rows by 2 inner block indices) at most 8 blocks are stored; the shard of the first 16 block rows and first 2 inner indices stores exactly 8.
All inputs are finite; a program needn't handle non-finite values.
Results may differ from a plain program's by a relative error of at most 0.00007.
Values sent between devices are 32-bit elements; how exact they have to be, the bound alone decides.
No kernel may reach another device: no remote copies, remote signals or barrier semaphores. Data moves between devices by JAX's collectives and lax.ppermute only.
A program may use at most 128 MiB of HBM per device.

v0:
```python
import jax
import jax.numpy as jnp
from jax import lax
from jax.sharding import PartitionSpec as P

BLOCK = 64


def expand(mask):
    return jnp.repeat(jnp.repeat(mask, BLOCK, axis=0), BLOCK, axis=1).astype(jnp.float32)


def shards(a_blocks, mask_a, b_blocks, mask_b):
    b_masked = b_blocks * expand(mask_b)
    b_whole = lax.all_gather(b_masked, "row", axis=0, tiled=True)
    a_masked = a_blocks * expand(mask_a)
    return jnp.dot(
        lax.all_gather(a_masked, ("col", "layer"), axis=1, tiled=True),
        b_whole,
        precision=lax.Precision.HIGHEST,
        preferred_element_type=jnp.float32,
    )


def solution(mesh):
    placed = (
        P("row", ("col", "layer")),
        P("row", ("col", "layer")),
        P("row", ("col", "layer")),
        P("row", ("col", "layer")),
    )
    return jax.shard_map(
        shards, mesh=mesh, in_specs=placed, out_specs=P("row", ("col", "layer")), check_vma=False
    )
```

profile of v0, /device:TPU:0, one launch (start us, length us, event | category | flops | bytes accessed | tf_op | source)
XLA Modules:
  0.0 391.2 jit_solution(702926884030204920)
XLA Ops:
  6.5 0.0 copy-start
  6.5 0.0 copy-start.1
  6.5 0.0 all-gather.5.cloned.1.call-start
  6.5 5.4 %copy.8 = f32[1024,1024]{0,1:T(8,128)} copy(f32[1024,1024]{1,0:T(8,128)} %param.6) | data formatting | bytes 8388608 | tf_op args[2]
  11.9 0.7 convert_element_type.25
  12.6 0.1 copy.7
  12.7 0.1 broadcast_in_dim.14
  12.8 0.1 convert_element_type.26
  12.9 5.1 %bitcast_multiply_fusion = f32[1024,1024]{0,1:T(8,128)} fusion(f32[1024,1024]{0,1:T(8,128)} %copy.8, f32[1024,16]{0,1:T(8,128)S(1)} %convert_element_type.26), kind=kLoop, calls=%fused_computation | loop fusion | flops 1048576 | bytes 8454144 | tf_op jit(solution)/shard_map/mul | solution.py:14
  18.0 0.0 all-gather.5.cloned.1.call-update
  18.0 0.0 all-gather.3.cloned.1.call-start
  18.0 0.0 copy-done
  18.1 0.2 copy.6
  18.3 0.0 copy-done.1
  18.3 0.1 broadcast_in_dim.12
  18.4 0.1 convert_element_type.23
  18.4 0.9 bitcast_multiply_fusion.1
  19.3 0.0 all-gather.3.cloned.1.call-update
  19.3 155.3 %all-gather.5.cloned.1.call-done = f32[4096,1024]{0,1:T(8,128)} async-done(((f32[1024,1024]{0,1:T(8,128)}), f32[4096,1024]{0,1:T(8,128)}) %all-gather.5.cloned.1.call-update) | async-done | bytes 16777232 | tf_op jit(solution)/shard_map/all_gather | solution.py:15
  174.7 99.9 %all-gather.3.cloned.1.call-done = f32[1024,4096]{0,1:T(8,128)} async-done(((f32[1024,128]{0,1:T(8,128)}), f32[1024,4096]{0,1:T(8,128)}) %all-gather.3.cloned.1.call-update) | async-done | bytes 16777232 | tf_op jit(solution)/shard_map/all_gather | solution.py:18
  274.6 109.8 %fusion = f32[1024,1024]{1,0:T(8,128)} fusion(f32[1024,4096]{0,1:T(8,128)} %all-gather.3.cloned.1.call-done, f32[4096,1024]{0,1:T(8,128)} %all-gather.5.cloned.1.call-done), kind=kOutput, calls=%fused_computation.2 | convolution fusion | flops 51539607552 | bytes 37748736 | tf_op jit(solution)/shard_map/dot_general | solution.py:17
  (1 shorter events, 0.0 us)
Async XLA Ops:
  6.5 11.5 %copy-start = (f32[1024,128]{1,0:T(8,128)S(1)}, f32[1024,128]{1,0:T(8,128)}, u32[]{:S(2)}) copy-start(f32[1024,128]{1,0:T(8,128)} %param.4) | copy-start | bytes 1572868
  6.5 11.7 %copy-start.1 = (s32[16,2]{0,1:T(2,128)S(1)}, s32[16,2]{0,1:T(2,128)}, u32[]{:S(2)}) copy-start(s32[16,2]{0,1:T(2,128)} %param.5) | copy-start | bytes 388
  6.5 168.1 %all-gather.5.cloned.1.call-start = ((), (), s32[]{:S(2)}) async-start(), calls=%async_computation.1 | async-start | bytes 20971520 | tf_op jit(solution)/shard_map/all_gather | solution.py:15
  18.0 256.6 %all-gather.3.cloned.1.call-start = ((), (), s32[]{:S(2)}) async-start(), calls=%async_computation | async-start | bytes 17301504 | tf_op jit(solution)/shard_map/all_gather | solution.py:18
Sparse Core Ops, SparseCore 0:
  18.1 156.4 all-gather.4
  176.4 98.1 all-gather.2
where the time goes:
time: 393 us; the launch traced here: 391 us
  waiting for transfers between devices  255 us (65%)
  matrix products  110 us (28%)
  between operations  13.4 us (3%)
  other arithmetic  6.62 us (2%)
  local copies, waits for them, and re-layouts  6.02 us (2%)
    all_gather x1, waiting for transfers between devices, shards(): b_whole = lax.all_gather(b_masked, 'row', axis=0, tiled=True)  155 us
    dot_general x1, matrix products, shards(): jnp.dot(lax.all_gather(a_masked, ('col', 'layer'), axis=1, tiled=True), b...  110 us
    all_gather x1, waiting for transfers between devices, shards(): lax.all_gather(a_masked, ('col', 'layer'), axis=1, tiled=True)  99.9 us
  transfers between devices with their start and end apart: 2, of which 2 were waited for; matrix products, arithmetic and copies ran while one was open for 0% of the time, Pallas kernels for 0%

commit v1 on v0

v1 whole, which is shorter than its diff:
```python
import jax
import jax.numpy as jnp
from jax import lax
from jax.experimental import pallas as pl
from jax.experimental.pallas import tpu as pltpu
from jax.sharding import Mesh, PartitionSpec as P

BLOCK = 64
ROWS = 4
A_SLOTS = 8
A_TILES = A_SLOTS // 2
A_ROWS = 8 + A_TILES * BLOCK
B_SLOTS = 38
B_TILES = B_SLOTS // 2
B_ROWS = 8 + B_TILES * BLOCK
A_SHARDS = 32
A_PER_GROUP = 4
LHS_ROWS = (A_SHARDS * A_SLOTS + 4) * BLOCK
TAB = 512
TAB_START, TAB_COUNT, TAB_ROW, TAB_MOST = 0, 64, 128, 511
DUMP = 16
AXES = ("zl", "y", "zh", "core")
F32, BF16, I32 = jnp.float32, jnp.bfloat16, jnp.int32


def _lane(rows=1):
    return lax.broadcasted_iota(I32, (rows, 128), 1)


def _split_pair(left, right, odd_left, odd_right):
    a = jnp.where(odd_left == 1, pltpu.roll(left, 64, 1), left)
    b = jnp.where(odd_right == 1, right, pltpu.roll(right, 64, 1))
    return jnp.where(_lane(BLOCK) < 64, a, b)


def pack_kernel(round_ref, ma_ref, mb_ref, a_hbm, b_hbm, pa_ref, p0_ref, p1_ref, abuf, bbuf, ia, ib, sem):
    row = lax.axis_index("row")
    shard = lax.axis_index("zl") * 16 + lax.axis_index("y") * 4 + lax.axis_index("zh") * 2 + lax.axis_index("core")
    acopy = pltpu.make_async_copy(a_hbm, abuf, sem.at[0])
    bcopy = pltpu.make_async_copy(b_hbm, bbuf, sem.at[1])
    acopy.start()
    bcopy.start()

    for s in range(A_SLOTS):
        ia[s] = 0
    n = 0
    counts = []
    for k in range(2):
        for i in range(16):
            ia[n] = k * 16 + i
            n = n + ma_ref[i, k]
        counts.append(n)

    def clear(s, c):
        ib[s] = 0
        return c

    lax.fori_loop(0, 2 * B_SLOTS * 5, clear, 0, unroll=20)

    def scan_row(k, n):
        for j in range(16):
            ib[n] = k * 16 + j
            n = n + mb_ref[k, j]
        return n

    nb = lax.fori_loop(0, 16, scan_row, 0)
    ib[nb] = 0

    lane = _lane(8)
    acopy.wait()
    head = jnp.where(lane == 8, counts[0], jnp.where(lane == 9, counts[1] - counts[0], jnp.where(lane == 10, shard, 0)))
    for t in range(A_TILES):
        e0, e1 = ia[2 * t], ia[2 * t + 1]
        x0 = abuf[pl.ds(pl.multiple_of((e0 & 15) * BLOCK, BLOCK), BLOCK), :]
        x1 = abuf[pl.ds(pl.multiple_of((e1 & 15) * BLOCK, BLOCK), BLOCK), :]
        pa_ref[8 + t * BLOCK : 8 + (t + 1) * BLOCK, :] = _split_pair(x0, x1, e0 >> 4, e1 >> 4)
        head = jnp.where(lane == 2 * t, e0 & 15, jnp.where(lane == 2 * t + 1, e1 & 15, head))
    pa_ref[0:8, :] = head.astype(F32)

    bcopy.wait()
    first = round_ref[0] * (2 * B_SLOTS)
    for half, out in enumerate((p0_ref, p1_ref)):
        base = first + half * B_SLOTS

        def tile(t, head, base=base, out=out):
            s = base + 2 * t
            e0, e1 = ib[s], ib[s + 1]
            x0 = bbuf[pl.ds(pl.multiple_of((e0 >> 4) * BLOCK, BLOCK), BLOCK), pl.ds(pl.multiple_of(((e0 & 15) >> 1) * 128, 128), 128)]
            x1 = bbuf[pl.ds(pl.multiple_of((e1 >> 4) * BLOCK, BLOCK), BLOCK), pl.ds(pl.multiple_of(((e1 & 15) >> 1) * 128, 128), 128)]
            out[pl.ds(pl.multiple_of(8 + t * BLOCK, 8), BLOCK), :] = _split_pair(x0, x1, e0 & 1, e1 & 1)
            return jnp.where(lane == 2 * t, e0, jnp.where(lane == 2 * t + 1, e1, head))

        head = lax.fori_loop(0, B_TILES, tile, jnp.zeros((8, 128), I32), unroll=2)
        head = head + row * 256
        head = jnp.where(lane == 126, nb, head)
        head = jnp.where(lane == 127, jnp.clip(nb - base, 0, B_SLOTS), head)
        out[0:8, :] = head.astype(F32)


def pack(rnd, mask_a, mask_b, a, b):
    smem = pl.BlockSpec(memory_space=pltpu.SMEM)
    vmem = pl.BlockSpec(memory_space=pltpu.VMEM)
    hbm = pl.BlockSpec(memory_space=pl.ANY)
    return pl.pallas_call(
        pack_kernel,
        in_specs=[smem, smem, smem, hbm, hbm],
        out_specs=[vmem, vmem, vmem],
        out_shape=[
            jax.ShapeDtypeStruct((A_ROWS, 128), F32),
            jax.ShapeDtypeStruct((B_ROWS, 128), F32),
            jax.ShapeDtypeStruct((B_ROWS, 128), F32),
        ],
        scratch_shapes=[
            pltpu.VMEM(a.shape, F32),
            pltpu.VMEM(b.shape, F32),
            pltpu.SMEM((64,), I32),
            pltpu.SMEM((512,), I32),
            pltpu.SemaphoreType.DMA((2,)),
        ],
        compiler_params=pltpu.CompilerParams(vmem_limit_bytes=12 << 20),
        name="pack",
    )(rnd, mask_a, mask_b, a, b)


def product_kernel(*refs, n_half, first):
    n_a = A_SHARDS // A_PER_GROUP
    if first:
        a_hbm, refs = refs[:n_a], refs[n_a:]
    else:
        lhs_in, tab_in, c_in, refs = refs[0], refs[1], refs[2], refs[3:]
    b_hbm, refs = refs[:n_half], refs[n_half:]
    if first:
        c_out, lhs_out, tab, refs = refs[0], refs[1], refs[2], refs[3:]
        abuf, ahead, refs = refs[0], refs[1], refs[2:]
    else:
        c_out, most_out, refs = refs[0], refs[1], refs[2:]
        tab = tab_in
    lhs, c, bbuf, bhead, rhs, tk, tj, wt, ws, wn, sem = refs

    body_copies, head_copies = [], []
    for h in range(n_half):
        head_copies.append(pltpu.make_async_copy(b_hbm[h].at[pl.ds(0, 8), :], bhead.at[h], sem.at[0, h]))
        body_copies.append(pltpu.make_async_copy(b_hbm[h].at[pl.ds(8, B_ROWS - 8), :], bbuf.at[h], sem.at[1, h]))
    if first:
        a_copies, a_heads = [], []
        for g in range(n_a):
            a_copies.append(pltpu.make_async_copy(a_hbm[g], abuf.at[pl.ds(g * A_PER_GROUP * A_ROWS, A_PER_GROUP * A_ROWS), :], sem.at[2, g]))
            for q in range(A_PER_GROUP):
                a_heads.append(pltpu.make_async_copy(a_hbm[g].at[pl.ds(q * A_ROWS, 8), :], ahead.at[g * A_PER_GROUP + q], sem.at[3, g * A_PER_GROUP + q]))
        for copy in a_heads + a_copies:
            copy.start()
    else:
        lhs_copy = pltpu.make_async_copy(lhs_in, lhs, sem.at[2, 0])
        c_copy = pltpu.make_async_copy(c_in, c.at[pl.ds(0, 1024), :], sem.at[2, 1])
        lhs_copy.start()
        c_copy.start()
    for copy in head_copies + body_copies:
        copy.start()

    low = _lane(BLOCK) < 64

    def halves(x):
        hi = x.astype(BF16).astype(F32)
        return hi, x - hi

    if first:
        c[0:1024, :] = jnp.zeros((1024, 1024), F32)

        for g in range(n_a):
            for q in range(A_PER_GROUP):
                a_heads[g * A_PER_GROUP + q].wait()
            a_copies[g].wait()

            def shard(q, carry):
                head = ahead.at[q]
                n0 = head[0, 8].astype(I32)
                n1 = head[0, 9].astype(I32)
                at = head[0, 10].astype(I32)
                tab[TAB_START + 2 * at] = 8 * q
                tab[TAB_START + 2 * at + 1] = 8 * q + n0
                tab[TAB_COUNT + 2 * at] = n0
                tab[TAB_COUNT + 2 * at + 1] = n1
                for s in range(A_SLOTS):
                    tab[TAB_ROW + 8 * q + s] = head[0, s].astype(I32)
                for t in range(A_TILES):
                    x = abuf[pl.ds(pl.multiple_of(q * A_ROWS + 8 + t * BLOCK, 8), BLOCK), :]
                    swapped = pltpu.roll(x, 64, 1)
                    for p in range(2):
                        hi, lo = halves(jnp.where(low, x, swapped) if p == 0 else jnp.where(low, swapped, x))
                        lhs[pl.ds(pl.multiple_of((8 * q + 2 * t + p) * BLOCK, BLOCK), BLOCK), :] = jnp.where(low, hi, lo).astype(BF16)
                return carry

            lax.fori_loop(g * A_PER_GROUP, (g + 1) * A_PER_GROUP, shard, 0)
        for s in range(4):
            tab[TAB_ROW + A_SHARDS * A_SLOTS + s] = DUMP
        lhs_copy = pltpu.make_async_copy(lhs, lhs_out, sem.at[2, n_a])
        lhs_copy.start()

    most = I32(0) if first else tab[TAB_MOST]
    for h in range(n_half):
        head_copies[h].wait()
        body_copies[h].wait()
        head, body = bhead.at[h], bbuf.at[h]
        most = jnp.maximum(most, head[0, 126].astype(I32))
        n = head[0, 127].astype(I32)

        def unpack(s, carry):
            t, par, before, w, v = carry
            e = head[0, s].astype(I32)
            pair = e >> 1
            k = e >> 4
            new = pair != before
            new_k = k != (before >> 3)
            x = body[pl.ds(pl.multiple_of((s >> 1) * BLOCK, BLOCK), BLOCK), :]
            x = jnp.where(((s ^ e) & 1) == 1, pltpu.roll(x, 64, 1), x)
            v = jnp.where((_lane(BLOCK) >> 6) == (e & 1), x, jnp.where(new, 0.0, v))
            hi, lo = halves(v)
            t = t + new.astype(I32)
            rhs[pl.ds(pl.multiple_of(t * 128, 128), BLOCK), :] = hi.astype(BF16)
            rhs[pl.ds(pl.multiple_of(t * 128 + BLOCK, BLOCK), BLOCK), :] = lo.astype(BF16)
            par = jnp.where(new, jnp.where(new_k, 0, 1 - par), par)
            tk[t] = k
            tj[t] = pair & 7
            emit = jnp.logical_and(new, par == 0)
            nk = tab[TAB_COUNT + k]
            start = tab[TAB_START + k]
            wt[w] = t
            ws[w] = start
            wn[w] = jnp.minimum(nk, 4)
            w = w + jnp.logical_and(emit, nk > 0).astype(I32)
            wt[w] = t
            ws[w] = start + 4
            wn[w] = nk - 4
            w = w + jnp.logical_and(emit, nk > 4).astype(I32)
            return t, par, pair, w, v

        t, _, _, work, _ = lax.fori_loop(0, n, unpack, (I32(-1), I32(0), I32(-8), I32(0), jnp.zeros((BLOCK, 128), F32)))
        tk[t + 1] = -1
        tj[t + 1] = 0
        wt[work] = 0
        ws[work] = 0
        wn[work] = 0

        if not first and h == 0:
            lhs_copy.wait()
            c_copy.wait()

        def multiply(m, carry):
            results = []
            for u in range(2):
                w = 2 * m + u
                t, s = wt[w], ws[w]
                left = lhs[pl.ds(pl.multiple_of(s * BLOCK, BLOCK), 4 * BLOCK), :]
                cols = []
                for p in range(2):
                    tile = rhs[pl.ds(pl.multiple_of((t + p) * 128, 128), 128), :]
                    cols.append(jnp.concatenate([tile[:BLOCK], tile[:BLOCK], tile[BLOCK:], tile[BLOCK:]], axis=0))
                results.append(
                    jnp.dot(
                        jnp.concatenate([left, left], axis=1),
                        jnp.concatenate(cols, axis=1),
                        preferred_element_type=F32,
                    )
                )
            for u in range(2):
                w = 2 * m + u
                t, s, n = wt[w], ws[w], wn[w]
                both = tk[t + 1] == tk[t]
                for p in range(2):
                    col = pl.ds(pl.multiple_of(tj[t + p] * 128, 128), 128)
                    for q in range(4):
                        i = jnp.where(q < n, tab[TAB_ROW + s + q], DUMP)
                        if p == 1:
                            i = jnp.where(both, i, DUMP)
                        rows = pl.ds(pl.multiple_of(i * BLOCK, BLOCK), BLOCK)
                        c[rows, col] = c[rows, col] + results[u][q * BLOCK : (q + 1) * BLOCK, p * 128 : (p + 1) * 128]
            return carry

        lax.fori_loop(0, (work + 1) // 2, multiply, 0)

    if first:
        tab[TAB_MOST] = most
    else:
        most_out[0] = most
    out_copy = pltpu.make_async_copy(c.at[pl.ds(0, 1024), :], c_out, sem.at[3, A_SHARDS])
    out_copy.start()
    if first:
        lhs_copy.wait()
    out_copy.wait()


def product(a_parts, state, halves):
    first = state is None
    n_half = len(halves)
    smem = pl.BlockSpec(memory_space=pltpu.SMEM)
    hbm = pl.BlockSpec(memory_space=pl.ANY)
    c_type = jax.ShapeDtypeStruct((1024, 1024), F32)
    lhs_type = jax.ShapeDtypeStruct((LHS_ROWS, 128), BF16)
    tab_type = jax.ShapeDtypeStruct((TAB,), I32)
    scratch = [
        pltpu.VMEM((LHS_ROWS, 128), BF16),
        pltpu.VMEM((1024 + BLOCK, 1024), F32),
        pltpu.VMEM((n_half, B_ROWS - 8, 128), F32),
        pltpu.SMEM((n_half, 8, 128), F32),
        pltpu.VMEM(((B_SLOTS + 2) * 128, 128), BF16),
        pltpu.SMEM((64,), I32),
        pltpu.SMEM((64,), I32),
        pltpu.SMEM((128,), I32),
        pltpu.SMEM((128,), I32),
        pltpu.SMEM((128,), I32),
        pltpu.SemaphoreType.DMA((4, A_SHARDS + 1)),
    ]
    params = pltpu.CompilerParams(vmem_limit_bytes=24 << 20)
    if first:
        args = tuple(a_parts) + tuple(halves)
        scratch = [pltpu.VMEM((A_SHARDS * A_ROWS, 128), F32), pltpu.SMEM((A_SHARDS, 8, 128), F32)] + scratch
        in_specs = [hbm] * len(args)
        out_specs, out_shape, aliases = [hbm, hbm, smem], [c_type, lhs_type, tab_type], {}
    else:
        lhs, tab, c = state
        args = (lhs, tab, c) + tuple(halves)
        in_specs = [hbm, smem] + [hbm] * (len(args) - 2)
        out_specs, out_shape, aliases = [hbm, smem], [c_type, jax.ShapeDtypeStruct((1,), I32)], {2: 0}

    def kernel(*refs):
        product_kernel(*refs, n_half=n_half, first=first)

    return pl.pallas_call(
        kernel,
        in_specs=in_specs,
        out_specs=out_specs,
        out_shape=out_shape,
        input_output_aliases=aliases,
        scratch_shapes=scratch,
        compiler_params=params,
        name="product_first" if first else "product_more",
    )(*args)


def _flat(zl, y, zh, core):
    return ((zl * 4 + y) * 2 + zh) * 2 + core


def _turn(step, swapped):
    pairs = []
    for z in range(4):
        for y in range(4):
            for core in range(2):
                along_y = (core == 0) != swapped
                to_y, to_z = ((y + step) % 4, z) if along_y else (y, (z + step) % 4)
                pairs.append((_flat(z % 2, y, z // 2, core), _flat(to_z % 2, to_y, to_z // 2, core)))
    return pairs


def gather_a(packed):
    near = [packed] + [lax.ppermute(packed, AXES, _turn(s, False)) for s in (1, 3, 2)]
    group = jnp.concatenate(near, axis=0)
    mine = [group] + [lax.ppermute(group, AXES, _turn(s, True)) for s in (1, 3, 2)]
    other = [lax.ppermute(x, "core", [(0, 1), (1, 0)]) for x in mine]
    return mine + other


def ring_b(p0, p1):
    up = [(i, (i + 1) % ROWS) for i in range(ROWS)]
    down = [(i, (i - 1) % ROWS) for i in range(ROWS)]
    l0 = lax.ppermute(p0, "row", up)
    r1 = lax.ppermute(p1, "row", down)
    l1 = lax.ppermute(p1, "row", up)
    r0 = lax.ppermute(p0, "row", down)
    far0 = lax.ppermute(l0, "row", up)
    far1 = lax.ppermute(r1, "row", down)
    return (p0, p1, l0, r1, l1, r0), (far0, far1)


def shards(a_blocks, mask_a, b_blocks, mask_b):
    pa, p0, p1 = pack(jnp.zeros((1,), I32), mask_a, mask_b, a_blocks, b_blocks)
    near, far = ring_b(p0, p1)
    a_parts = gather_a(pa)
    c, lhs, tab = product(a_parts, None, near)
    c, most = product(None, (lhs, tab, c), far)
    most = most[0]

    def again(carry):
        r, c = carry
        _, p0, p1 = pack(r[None], mask_a, mask_b, a_blocks, b_blocks)
        near, far = ring_b(p0, p1)
        return r + 1, product(None, (lhs, tab, c), near + far)[0]

    return lax.while_loop(lambda carry: carry[0] * (2 * B_SLOTS) < most, again, (I32(1), c))[1]


def solution(mesh):
    fine = Mesh(mesh.devices.reshape(4, 2, 4, 2, 2), ("row",) + AXES)
    placed = P("row", AXES)
    return jax.shard_map(shards, mesh=fine, in_specs=(placed,) * 4, out_specs=placed, check_vma=False)
```

time: 393 us -> 96 us (0.24)
  waiting for transfers between devices: 255 us -> 14.7 us
  matrix products: 110 us -> 0 us
  Pallas kernels: 0 us -> 49.1 us
  starting transfers between devices: 0.04 us -> 21.9 us
  between operations: 13.4 us -> 0.29 us
  other arithmetic: 6.62 us -> 0 us
    all_gather x2 -> x0, waiting for transfers between devices: 255 us -> none  [the longest x1 155 us: shards(): b_whole = lax.all_gather(b_masked, 'row', axis=0, tiled=True)]
    dot_general x1 -> x0, matrix products: 110 us -> none  [shards(): jnp.dot(lax.all_gather(a_masked, ('col', 'layer'), axis=1, tiled=True), b...]
    pallas_call x0 -> x3, Pallas kernels: none -> 49.1 us  [the longest x2 43.7 us: product(): pl.pallas_call(kernel, in_specs=in_specs, out_specs=out_specs, out_shape=...]
    ppermute x0 -> x16, starting transfers between devices: none -> 21.9 us  [the longest x3 6.13 us: gather_a(): lax.ppermute(group, AXES, _turn(s, True))]
    ppermute x0 -> x16, waiting for transfers between devices: none -> 14.7 us  [the longest x1 7.89 us: ring_b(): l1 = lax.ppermute(p1, 'row', up)]
    mul x2 -> x0, other arithmetic: 5.92 us -> none  [the longest x1 5.06 us: shards(): b_masked = b_blocks * expand(mask_b)]
    unnamed x6 -> x22, local copies, waits for them, and re-layouts: 5.6 us -> 8.48 us
  transfers between devices with their start and end apart: 2 -> 16, of which waited for: 2 -> 6; matrix products, arithmetic and copies ran while one was open for 0% -> 0% of each run, Pallas kernels for 0% -> 34%
where the time goes in v1:
time: 96 us; the launch traced here: 95.4 us
  Pallas kernels  49.1 us (51%)
  starting transfers between devices  21.9 us (23%)
  waiting for transfers between devices  14.7 us (15%)
  local copies, waits for them, and re-layouts  8.49 us (9%)
    pallas_call x2, Pallas kernels, product(): pl.pallas_call(kernel, in_specs=in_specs, out_specs=out_specs, out_shape=...  43.7 us
    unnamed x22, local copies, waits for them, and re-layouts  8.48 us
    ppermute x1, waiting for transfers between devices, ring_b(): l1 = lax.ppermute(p1, 'row', up)  7.89 us
    ppermute x3, starting transfers between devices, gather_a(): lax.ppermute(group, AXES, _turn(s, True))  6.13 us
    pallas_call x1, Pallas kernels, pack(): pl.pallas_call(pack_kernel, in_specs=[smem, smem, smem, hbm, hbm], out_sp...  5.42 us
    ppermute x3, starting transfers between devices, gather_a(): lax.ppermute(packed, AXES, _turn(s, False))  5.22 us
    ppermute x3, waiting for transfers between devices, gather_a(): lax.ppermute(packed, AXES, _turn(s, False))  4.44 us
    ppermute x1, starting transfers between devices, ring_b(): r0 = lax.ppermute(p0, 'row', down)  3.02 us
  transfers between devices with their start and end apart: 16, of which 6 were waited for; matrix products, arithmetic and copies ran while one was open for 0% of the time, Pallas kernels for 34%

profile of v1, /device:TPU:0, one launch (start us, length us, event | category | flops | bytes accessed | tf_op | source)
XLA Modules:
  0.0 95.4 jit_solution(5882580391320605814)
XLA Ops:
  0.0 0.8 copy.7.ma_ref
  0.8 5.4 %pack.2 = (f32[264,128]{1,0:T(8,128)S(1)}, f32[1224,128]{1,0:T(8,128)S(1)}, f32[1224,128]{1,0:T(8,128)S(1)}) custom-call(s32[1]{0:T(128)} %constant.4.clone.1.round_ref, s32[16,2]{1,0:T(8,128)S(1)} %copy.7.ma_ref, s32[16,16]{1,0:T(8,128)} %mb_ref.1, f32[1024,128]{1,0:T(8,128)} %a_hbm.1, f32[1024,1024]{1,0:T(8,128)} %b_hbm.1), custom_call_target="tpu_custom_call" | custom-call | tf_op jit(solution)/shard_map/pack/pallas_call | solution.py:104
  6.2 1.6 %collective-permute-start.16 = (f32[1224,128]{1,0:T(8,128)S(1)}, f32[1224,128]{1,0:T(8,128)S(1)}, u32[]{:S(2)}, u32[]{:S(2)}) collective-permute-start(f32[1224,128]{1,0:T(8,128)S(1)} %get-tuple-element.65.refs_8_), channel_id=1, source_target_pairs={{0,32},{32,64},{64,96},{96,0},{1,33},{33,65},{65,97},{97,1},{2,34}... | collective-permute-start | bytes 1880072 | tf_op jit(solution)/shard_map/ppermute | solution.py:366
  7.8 1.7 %collective-permute-start.17 = (f32[1224,128]{1,0:T(8,128)S(1)}, f32[1224,128]{1,0:T(8,128)S(1)}, u32[]{:S(2)}, u32[]{:S(2)}) collective-permute-start(f32[1224,128]{1,0:T(8,128)S(1)} %get-tuple-element.66.refs_9_), channel_id=1, source_target_pairs={{0,96},{32,0},{64,32},{96,64},{1,97},{33,1},{65,33},{97,65},{2,98}... | collective-permute-start | bytes 1880072 | tf_op jit(solution)/shard_map/ppermute | solution.py:367
  9.5 0.4 collective-permute-start.18
  9.9 1.6 %collective-permute-start.6 = (f32[264,128]{1,0:T(8,128)S(1)}, f32[264,128]{1,0:T(8,128)S(1)}, u32[]{:S(2)}, u32[]{:S(2)}) collective-permute-start(f32[264,128]{1,0:T(8,128)S(1)} %get-tuple-element.64), channel_id=1, source_target_pairs={{0,4},{1,17},{4,8},{5,21},{8,12},{9,25},{12,0},{13,29},{16,20},{17... | collective-permute-start | bytes 405512 | tf_op jit(solution)/shard_map/ppermute | solution.py:356
  11.4 1.7 %collective-permute-start.7 = (f32[264,128]{1,0:T(8,128)S(1)}, f32[264,128]{1,0:T(8,128)S(1)}, u32[]{:S(2)}, u32[]{:S(2)}) collective-permute-start(f32[264,128]{1,0:T(8,128)S(1)} %get-tuple-element.64), channel_id=1, source_target_pairs={{0,12},{1,19},{4,0},{5,23},{8,4},{9,27},{12,8},{13,31},{16,28},{17... | collective-permute-start | bytes 405512 | tf_op jit(solution)/shard_map/ppermute | solution.py:356
  13.1 3.0 %collective-permute-done.6 = f32[264,128]{1,0:T(8,128)S(1)} collective-permute-done((f32[264,128]{1,0:T(8,128)S(1)}, f32[264,128]{1,0:T(8,128)S(1)}, u32[]{:S(2)}, u32[]{:S(2)}) %collective-permute-start.6) | collective-permute-done | bytes 135200 | tf_op jit(solution)/shard_map/ppermute | solution.py:356
  16.1 2.0 %collective-permute-start.8 = (f32[264,128]{1,0:T(8,128)S(1)}, f32[264,128]{1,0:T(8,128)S(1)}, u32[]{:S(2)}, u32[]{:S(2)}) collective-permute-start(f32[264,128]{1,0:T(8,128)S(1)} %get-tuple-element.64), channel_id=1, source_target_pairs={{0,8},{1,3},{4,12},{5,7},{8,0},{9,11},{12,4},{13,15},{16,24},{17,1... | collective-permute-start | bytes 405512 | tf_op jit(solution)/shard_map/ppermute | solution.py:356
  18.1 3.0 %collective-permute-start.19 = (f32[1224,128]{1,0:T(8,128)S(1)}, f32[1224,128]{1,0:T(8,128)S(1)}, u32[]{:S(2)}, u32[]{:S(2)}) collective-permute-start(f32[1224,128]{1,0:T(8,128)S(1)} %get-tuple-element.65.refs_8_), channel_id=1, source_target_pairs={{0,96},{32,0},{64,32},{96,64},{1,97},{33,1},{65,33},{97,65},{2,98}... | collective-permute-start | bytes 1880072 | tf_op jit(solution)/shard_map/ppermute | solution.py:369
  21.1 1.5 %collective-permute-done.8 = f32[264,128]{1,0:T(8,128)S(1)} collective-permute-done((f32[264,128]{1,0:T(8,128)S(1)}, f32[264,128]{1,0:T(8,128)S(1)}, u32[]{:S(2)}, u32[]{:S(2)}) %collective-permute-start.8) | collective-permute-done | bytes 135200 | tf_op jit(solution)/shard_map/ppermute | solution.py:356
  22.6 2.0 %collective-permute-start.9 = (f32[1056,128]{1,0:T(8,128)S(1)}, f32[1056,128]{1,0:T(8,128)}, u32[]{:S(2)}, u32[]{:S(2)}) collective-permute-start(f32[1056,128]{1,0:T(8,128)S(1)} %constant_dynamic-update-slice_fusion.refs_0_), channel_id=1, source_target_pairs={{0,16},{1,5},{4,20},{5,9},{8,24},{9,13},{12,28},{13,1},{16,2},{17,... | collective-permute-start | bytes 1622024 | tf_op jit(solution)/shard_map/ppermute | solution.py:358
  24.6 4.0 %collective-permute-start.10 = (f32[1056,128]{1,0:T(8,128)S(1)}, f32[1056,128]{1,0:T(8,128)}, u32[]{:S(2)}, u32[]{:S(2)}) collective-permute-start(f32[1056,128]{1,0:T(8,128)S(1)} %constant_dynamic-update-slice_fusion.refs_0_), channel_id=1, source_target_pairs={{0,18},{1,13},{4,22},{5,1},{8,26},{9,5},{12,30},{13,9},{16,0},{17,... | collective-permute-start | bytes 1622024 | tf_op jit(solution)/shard_map/ppermute | solution.py:358
  28.6 0.2 collective-permute-start.11
  28.8 7.9 %collective-permute-done.18.refs_12_ = f32[1224,128]{1,0:T(8,128)S(1)} collective-permute-done((f32[1224,128]{1,0:T(8,128)S(1)}, f32[1224,128]{1,0:T(8,128)S(1)}, u32[]{:S(2)}, u32[]{:S(2)}) %collective-permute-start.18) | collective-permute-done | bytes 626720 | tf_op jit(solution)/shard_map/ppermute | solution.py:368
  36.6 0.8 copy-done
  37.5 0.8 copy-done.2
  38.3 0.8 collective-permute-start.20
  39.2 2.4 %collective-permute-start.21 = (f32[1224,128]{1,0:T(8,128)S(1)}, f32[1224,128]{1,0:T(8,128)}, u32[]{:S(2)}, u32[]{:S(2)}) collective-permute-start(f32[1224,128]{1,0:T(8,128)S(1)} %collective-permute-done.17.refs_11_), channel_id=1, source_target_pairs={{0,96},{32,0},{64,32},{96,64},{1,97},{33,1},{65,33},{97,65},{2,98}... | collective-permute-start | bytes 1880072 | tf_op jit(solution)/shard_map/ppermute | solution.py:371
  41.6 0.5 collective-permute-start.14
  42.1 0.8 copy-done.4
  42.9 0.1 collective-permute-start.15
  43.0 0.8 collective-permute-done.13.refs_5_
  43.8 0.8 collective-permute-done.14.refs_6_
  44.6 0.8 collective-permute-done.15.refs_7_
  45.4 1.1 %copy-done.1 = f32[1224,128]{1,0:T(8,128)S(1)} copy-done((f32[1224,128]{1,0:T(8,128)S(1)}, f32[1224,128]{1,0:T(8,128)}, u32[]{:S(2)}) %copy-start.1) | copy-done | bytes 626712
  46.5 1.1 %copy-done.3 = f32[1224,128]{1,0:T(8,128)S(1)} copy-done((f32[1224,128]{1,0:T(8,128)S(1)}, f32[1224,128]{1,0:T(8,128)}, u32[]{:S(2)}) %copy-start.3) | copy-done | bytes 626712
  47.5 1.0 %copy-done.5 = f32[1056,128]{1,0:T(8,128)S(1)} copy-done((f32[1056,128]{1,0:T(8,128)S(1)}, f32[1056,128]{1,0:T(8,128)}, u32[]{:S(2)}) %copy-start.5) | copy-done | bytes 540696
  48.6 32.4 %product_first.1 = (f32[1024,1024]{1,0:T(8,128)S(1)}, bf16[16640,128]{1,0:T(8,128)(2,1)S(1)}, s32[512]{0:T(512)S(1)}) custom-call(f32[1056,128]{1,0:T(8,128)S(1)} %constant_dynamic-update-slice_fusion.refs_0_, f32[1056,128]{1,0:T(8,128)} %collective-permute-done.9.refs_1_, f32[1056,128]{1,0:T(8,128)} %collective-permute-done.10.refs_2_, ...), custom_call_target="tpu_custom_call" | custom-call | tf_op jit(solution)/shard_map/product_first/pallas_call | solution.py:328
  81.0 11.4 %product_more.2 = (f32[1024,1024]{1,0:T(8,128)S(1)}, s32[1]{0:T(128)}) custom-call(bf16[16640,128]{1,0:T(8,128)(2,1)S(1)} %get-tuple-element.169.refs_0_, s32[512]{0:T(512)S(1)} %get-tuple-element.170.refs_1_, f32[1024,1024]{1,0:T(8,128)S(1)} %get-tuple-element.69.refs_2_, ...), custom_call_target="tpu_custom_call", output_to_operand_aliasing={{0}: (2, {})} | custom-call | tf_op jit(solution)/shard_map/product_more/pallas_call | solution.py:328
  92.4 2.0 %copy-done.7 = f32[1024,1024]{1,0:T(8,128)} copy-done((f32[1024,1024]{1,0:T(8,128)}, f32[1024,1024]{1,0:T(8,128)S(1)}, u32[]{:S(2)}) %copy-start.7) | copy-done | bytes 4194328
  94.4 0.8 while.10
  (27 shorter events, 0.1 us)
Async XLA Ops:
  6.2 18.4 %collective-permute-start.16 = (f32[1224,128]{1,0:T(8,128)S(1)}, f32[1224,128]{1,0:T(8,128)S(1)}, u32[]{:S(2)}, u32[]{:S(2)}) collective-permute-start(f32[1224,128]{1,0:T(8,128)S(1)} %get-tuple-element.65.refs_8_), channel_id=1, source_target_pairs={{0,32},{32,64},{64,96},{96,0},{1,33},{33,65},{65,97},{97,1},{2,34}... | collective-permute-start | bytes 1880072 | tf_op jit(solution)/shard_map/ppermute | solution.py:366
  7.8 20.8 %collective-permute-start.17 = (f32[1224,128]{1,0:T(8,128)S(1)}, f32[1224,128]{1,0:T(8,128)S(1)}, u32[]{:S(2)}, u32[]{:S(2)}) collective-permute-start(f32[1224,128]{1,0:T(8,128)S(1)} %get-tuple-element.66.refs_9_), channel_id=1, source_target_pairs={{0,96},{32,0},{64,32},{96,64},{1,97},{33,1},{65,33},{97,65},{2,98}... | collective-permute-start | bytes 1880072 | tf_op jit(solution)/shard_map/ppermute | solution.py:367
  9.5 27.2 %collective-permute-start.18 = (f32[1224,128]{1,0:T(8,128)S(1)}, f32[1224,128]{1,0:T(8,128)S(1)}, u32[]{:S(2)}, u32[]{:S(2)}) collective-permute-start(f32[1224,128]{1,0:T(8,128)S(1)} %get-tuple-element.66.refs_9_), channel_id=1, source_target_pairs={{0,32},{32,64},{64,96},{96,0},{1,33},{33,65},{65,97},{97,1},{2,34}... | collective-permute-start | bytes 1880072 | tf_op jit(solution)/shard_map/ppermute | solution.py:368
  9.9 6.2 %collective-permute-start.6 = (f32[264,128]{1,0:T(8,128)S(1)}, f32[264,128]{1,0:T(8,128)S(1)}, u32[]{:S(2)}, u32[]{:S(2)}) collective-permute-start(f32[264,128]{1,0:T(8,128)S(1)} %get-tuple-element.64), channel_id=1, source_target_pairs={{0,4},{1,17},{4,8},{5,21},{8,12},{9,25},{12,0},{13,29},{16,20},{17... | collective-permute-start | bytes 405512 | tf_op jit(solution)/shard_map/ppermute | solution.py:356
  11.4 6.6 %collective-permute-start.7 = (f32[264,128]{1,0:T(8,128)S(1)}, f32[264,128]{1,0:T(8,128)S(1)}, u32[]{:S(2)}, u32[]{:S(2)}) collective-permute-start(f32[264,128]{1,0:T(8,128)S(1)} %get-tuple-element.64), channel_id=1, source_target_pairs={{0,12},{1,19},{4,0},{5,23},{8,4},{9,27},{12,8},{13,31},{16,28},{17... | collective-permute-start | bytes 405512 | tf_op jit(solution)/shard_map/ppermute | solution.py:356
  16.1 6.5 %collective-permute-start.8 = (f32[264,128]{1,0:T(8,128)S(1)}, f32[264,128]{1,0:T(8,128)S(1)}, u32[]{:S(2)}, u32[]{:S(2)}) collective-permute-start(f32[264,128]{1,0:T(8,128)S(1)} %get-tuple-element.64), channel_id=1, source_target_pairs={{0,8},{1,3},{4,12},{5,7},{8,0},{9,11},{12,4},{13,15},{16,24},{17,1... | collective-permute-start | bytes 405512 | tf_op jit(solution)/shard_map/ppermute | solution.py:356
  18.1 19.4 %collective-permute-start.19 = (f32[1224,128]{1,0:T(8,128)S(1)}, f32[1224,128]{1,0:T(8,128)S(1)}, u32[]{:S(2)}, u32[]{:S(2)}) collective-permute-start(f32[1224,128]{1,0:T(8,128)S(1)} %get-tuple-element.65.refs_8_), channel_id=1, source_target_pairs={{0,96},{32,0},{64,32},{96,64},{1,97},{33,1},{65,33},{97,65},{2,98}... | collective-permute-start | bytes 1880072 | tf_op jit(solution)/shard_map/ppermute | solution.py:369
  22.6 16.6 %collective-permute-start.9 = (f32[1056,128]{1,0:T(8,128)S(1)}, f32[1056,128]{1,0:T(8,128)}, u32[]{:S(2)}, u32[]{:S(2)}) collective-permute-start(f32[1056,128]{1,0:T(8,128)S(1)} %constant_dynamic-update-slice_fusion.refs_0_), channel_id=1, source_target_pairs={{0,16},{1,5},{4,20},{5,9},{8,24},{9,13},{12,28},{13,1},{16,2},{17,... | collective-permute-start | bytes 1622024 | tf_op jit(solution)/shard_map/ppermute | solution.py:358
  24.6 17.0 %collective-permute-start.10 = (f32[1056,128]{1,0:T(8,128)S(1)}, f32[1056,128]{1,0:T(8,128)}, u32[]{:S(2)}, u32[]{:S(2)}) collective-permute-start(f32[1056,128]{1,0:T(8,128)S(1)} %constant_dynamic-update-slice_fusion.refs_0_), channel_id=1, source_target_pairs={{0,18},{1,13},{4,22},{5,1},{8,26},{9,5},{12,30},{13,9},{16,0},{17,... | collective-permute-start | bytes 1622024 | tf_op jit(solution)/shard_map/ppermute | solution.py:358
  28.6 13.0 %collective-permute-start.11 = (f32[1056,128]{1,0:T(8,128)S(1)}, f32[1056,128]{1,0:T(8,128)}, u32[]{:S(2)}, u32[]{:S(2)}) collective-permute-start(f32[1056,128]{1,0:T(8,128)S(1)} %constant_dynamic-update-slice_fusion.refs_0_), channel_id=1, source_target_pairs={{0,2},{1,9},{4,6},{5,13},{8,10},{9,1},{12,14},{13,5},{16,18},{17,2... | collective-permute-start | bytes 1622024 | tf_op jit(solution)/shard_map/ppermute | solution.py:358
  36.6 0.8 copy-start
  37.5 4.6 %collective-permute-start.12 = (f32[1056,128]{1,0:T(8,128)S(1)}, f32[1056,128]{1,0:T(8,128)S(1)}, u32[]{:S(2)}, u32[]{:S(2)}) collective-permute-start(f32[1056,128]{1,0:T(8,128)S(1)} %constant_dynamic-update-slice_fusion.refs_0_), channel_id=1, source_target_pairs={{0,1},{1,0},{2,3},{3,2},{4,5},{5,4},{6,7},{7,6},{8,9},{9,8},{10,11... | collective-permute-start | bytes 1622024 | tf_op jit(solution)/shard_map/ppermute | solution.py:359
  37.5 0.8 copy-start.2
  38.3 42.6 %collective-permute-start.20 = (f32[1224,128]{1,0:T(8,128)S(1)}, f32[1224,128]{1,0:T(8,128)}, u32[]{:S(2)}, u32[]{:S(2)}) collective-permute-start(f32[1224,128]{1,0:T(8,128)S(1)} %collective-permute-done.16.refs_10_), channel_id=1, source_target_pairs={{0,32},{32,64},{64,96},{96,0},{1,33},{33,65},{65,97},{97,1},{2,34}... | collective-permute-start | bytes 1880072 | tf_op jit(solution)/shard_map/ppermute | solution.py:370
  39.2 41.8 %collective-permute-start.21 = (f32[1224,128]{1,0:T(8,128)S(1)}, f32[1224,128]{1,0:T(8,128)}, u32[]{:S(2)}, u32[]{:S(2)}) collective-permute-start(f32[1224,128]{1,0:T(8,128)S(1)} %collective-permute-done.17.refs_11_), channel_id=1, source_target_pairs={{0,96},{32,0},{64,32},{96,64},{1,97},{33,1},{65,33},{97,65},{2,98}... | collective-permute-start | bytes 1880072 | tf_op jit(solution)/shard_map/ppermute | solution.py:371
  41.6 2.3 %collective-permute-start.13 = (f32[1056,128]{1,0:T(8,128)}, f32[1056,128]{1,0:T(8,128)}, u32[]{:S(2)}, u32[]{:S(2)}) collective-permute-start(f32[1056,128]{1,0:T(8,128)} %collective-permute-done.9.refs_1_), channel_id=1, source_target_pairs={{0,1},{1,0},{2,3},{3,2},{4,5},{5,4},{6,7},{7,6},{8,9},{9,8},{10,11... | collective-permute-start | bytes 1622024 | tf_op jit(solution)/shard_map/ppermute | solution.py:359
  41.6 3.0 %collective-permute-start.14 = (f32[1056,128]{1,0:T(8,128)}, f32[1056,128]{1,0:T(8,128)}, u32[]{:S(2)}, u32[]{:S(2)}) collective-permute-start(f32[1056,128]{1,0:T(8,128)} %collective-permute-done.10.refs_2_), channel_id=1, source_target_pairs={{0,1},{1,0},{2,3},{3,2},{4,5},{5,4},{6,7},{7,6},{8,9},{9,8},{10,11... | collective-permute-start | bytes 1622024 | tf_op jit(solution)/shard_map/ppermute | solution.py:359
  42.1 0.8 copy-start.4
  42.9 2.5 %collective-permute-start.15 = (f32[1056,128]{1,0:T(8,128)}, f32[1056,128]{1,0:T(8,128)}, u32[]{:S(2)}, u32[]{:S(2)}) collective-permute-start(f32[1056,128]{1,0:T(8,128)} %collective-permute-done.11.refs_3_), channel_id=1, source_target_pairs={{0,1},{1,0},{2,3},{3,2},{4,5},{5,4},{6,7},{7,6},{8,9},{9,8},{10,11... | collective-permute-start | bytes 1622024 | tf_op jit(solution)/shard_map/ppermute | solution.py:359
  45.4 1.1 %copy-start.1 = (f32[1224,128]{1,0:T(8,128)S(1)}, f32[1224,128]{1,0:T(8,128)}, u32[]{:S(2)}) copy-start(f32[1224,128]{1,0:T(8,128)} %copy-done) | copy-start | bytes 1880068
  46.5 1.1 %copy-start.3 = (f32[1224,128]{1,0:T(8,128)S(1)}, f32[1224,128]{1,0:T(8,128)}, u32[]{:S(2)}) copy-start(f32[1224,128]{1,0:T(8,128)} %copy-done.2) | copy-start | bytes 1880068
  47.5 1.0 %copy-start.5 = (f32[1056,128]{1,0:T(8,128)S(1)}, f32[1056,128]{1,0:T(8,128)}, u32[]{:S(2)}) copy-start(f32[1056,128]{1,0:T(8,128)} %copy-done.4) | copy-start | bytes 1622020
  80.9 11.4 %copy-start.6 = (bf16[16640,128]{1,0:T(8,128)(2,1)}, bf16[16640,128]{1,0:T(8,128)(2,1)S(1)}, u32[]{:S(2)}) copy-start(bf16[16640,128]{1,0:T(8,128)(2,1)S(1)} %get-tuple-element.169.refs_0_) | copy-start | bytes 12779524
  81.0 13.4 %copy-start.8 = (s32[16,16]{1,0:T(8,128)S(1)}, s32[16,16]{1,0:T(8,128)}, u32[]{:S(2)}) copy-start(s32[16,16]{1,0:T(8,128)} %mb_ref.1) | copy-start | bytes 3076
  92.4 2.0 %copy-start.7 = (f32[1024,1024]{1,0:T(8,128)}, f32[1024,1024]{1,0:T(8,128)S(1)}, u32[]{:S(2)}) copy-start(f32[1024,1024]{1,0:T(8,128)S(1)} %get-tuple-element.163) | copy-start | bytes 12582916

commit v2 on v0

v2 whole, which is shorter than its diff:
```python
import jax
import jax.numpy as jnp
from jax import lax
from jax.experimental import pallas as pl
from jax.experimental.pallas import tpu as pltpu
from jax.sharding import Mesh, PartitionSpec as P

BLOCK = 64
ROWS = 4
A_SLOTS = 8
A_TILES = A_SLOTS // 2
A_ROWS = 8 + A_TILES * BLOCK
B_SLOTS = 38
B_TILES = B_SLOTS // 2
B_ROWS = 8 + B_TILES * BLOCK
MESSAGES = 8
H_K, H_J0, H_J1, H_L0, H_R0, H_L1, H_R1, H_COUNT = range(8)
E_STRIDE = 44
UNROLL = 6
UNPACK = 4
A_SHARDS = 32
A_PER_GROUP = 4
GROUPS = 96
TAB = 1024
TAB_GROUP, TAB_GROUPS, TAB_ROW = 0, 64, 128
C_TILES = 17 * 8
DUMP = 16 * 8
AXES = ("zl", "y", "zh", "core")
F32, BF16, I32 = jnp.float32, jnp.bfloat16, jnp.int32


def _cost(us):
    return pl.CostEstimate(flops=0, transcendentals=0, bytes_accessed=us * 3_690_000)


def _lane(rows=1):
    return lax.broadcasted_iota(I32, (rows, 128), 1)


def _side_by_side(left, right, odd_left, odd_right, keep=None):
    left, right = left.reshape(8, 8, 128), right.reshape(8, 8, 128)
    lane = lax.broadcasted_iota(I32, (1, 8, 128), 2)
    low = lane < 64
    turned = jnp.where(low, odd_left, 1 - odd_right) == 1
    far = pltpu.roll(jnp.where(low, right, left), 64, 2)
    both = jnp.where(turned, far, jnp.where(low, left, right))
    if keep is not None:
        both = jnp.where(jnp.logical_and(lane >= keep[0], lane < keep[1]), both, 0.0)
    return both.reshape(BLOCK, 128)


def pack_a_kernel(mask_ref, a_ref, out_ref, stored):
    shard = lax.axis_index("zl") * 16 + lax.axis_index("y") * 4 + lax.axis_index("zh") * 2 + lax.axis_index("core")
    for s in range(A_SLOTS):
        stored[s] = 0
    n = 0
    counts = []
    for k in range(2):
        for i in range(16):
            stored[n] = k * 16 + i
            n = n + mask_ref[k, i]
        counts.append(n)
    lane = _lane(8)
    head = jnp.where(lane == 8, counts[0], jnp.where(lane == 9, counts[1] - counts[0], jnp.where(lane == 10, shard, 0)))
    for t in range(A_TILES):
        e0, e1 = stored[2 * t], stored[2 * t + 1]
        x0 = a_ref[pl.ds(pl.multiple_of((e0 & 15) * BLOCK, BLOCK), BLOCK), :]
        x1 = a_ref[pl.ds(pl.multiple_of((e1 & 15) * BLOCK, BLOCK), BLOCK), :]
        out_ref[8 + t * BLOCK : 8 + (t + 1) * BLOCK, :] = _side_by_side(x0, x1, e0 >> 4, e1 >> 4)
        head = jnp.where(lane == 2 * t, e0 & 15, jnp.where(lane == 2 * t + 1, e1 & 15, head))
    out_ref[0:8, :] = head.astype(F32)


def pack_a(mask_a, a):
    return pl.pallas_call(
        pack_a_kernel,
        in_specs=[pl.BlockSpec(memory_space=pltpu.SMEM), pl.BlockSpec(memory_space=pltpu.VMEM)],
        out_specs=pl.BlockSpec(memory_space=pltpu.VMEM),
        out_shape=jax.ShapeDtypeStruct((A_ROWS, 128), F32),
        scratch_shapes=[pltpu.SMEM((64,), I32)],
        cost_estimate=_cost(2),
        name="pack_a",
    )(mask_a.T, a)


def pack_b_kernel(round_ref, mask_ref, b_hbm, after_ref, out, token, b, heads, source, size, headv, sem):
    copies = []
    for q in range(4):
        part = pl.ds(q * 256, 256)
        copies.append(pltpu.make_async_copy(b_hbm.at[part, :], b.at[part, :], sem.at[q]))
        copies[-1].start()
    row = lax.axis_index("row")
    for m in range(MESSAGES):
        size[m] = 0
        heads[m, H_COUNT, 0] = 0

    def scan_row(k, carry):
        m, e, n = carry
        par = I32(0)
        for j in range(8):
            m0, m1 = mask_ref[k, 2 * j], mask_ref[k, 2 * j + 1]
            count = m0 + m1
            full = n + count > B_SLOTS
            m = m + full.astype(I32)
            e = jnp.where(full, 0, e)
            n = jnp.where(full, 0, n)
            par = jnp.where(full, 0, par)
            at = e - par
            heads[m, H_K, at] = row * 16 + k
            heads[m, H_J0 + par, at] = j
            heads[m, H_J1, at] = j
            heads[m, H_L1, at] = -1
            heads[m, H_R1, at] = -1
            heads[m, H_L0 + 2 * par, at] = jnp.where(m0 == 1, n, -1)
            heads[m, H_R0 + 2 * par, at] = jnp.where(m1 == 1, n + m0, -1)
            source[m, n] = k * 16 + 2 * j
            source[m, n + m0] = k * 16 + 2 * j + 1
            some = jnp.minimum(count, 1)
            n = n + count
            e = e + some * (1 - par)
            par = par ^ some
            size[m] = n
            heads[m, H_COUNT, 0] = e
        return m, e, n

    last, _, _ = lax.fori_loop(0, 16, scan_row, (I32(0), I32(0), I32(0)))
    token[0] = last
    first = round_ref[0] * 2
    head_copies = []
    for half in range(2):
        heads[first + half, H_COUNT, 1] = last + 1
        head_copies.append(pltpu.make_async_copy(heads.at[first + half], headv.at[half], sem.at[4 + half]))
        head_copies[-1].start()
    for copy in copies:
        copy.wait()
    for half in range(2):
        m = first + half
        n = size[m]

        def some(g, carry, m=m, n=n, half=half):
            tiles = []
            for u in range(4):
                t = jnp.minimum(4 * g + u, B_TILES - 1)
                blocks = []
                for e in (source[m, jnp.minimum(2 * t, n - 1)], source[m, jnp.minimum(2 * t + 1, n - 1)]):
                    rows = pl.ds(pl.multiple_of((e >> 4) * BLOCK, BLOCK), BLOCK)
                    blocks.append((b[rows, pl.ds(pl.multiple_of(((e & 15) >> 1) * 128, 128), 128)], e & 1))
                tiles.append((t, _side_by_side(blocks[0][0], blocks[1][0], blocks[0][1], blocks[1][1])))
            for t, tile in tiles:
                out[pl.ds(pl.multiple_of(half * B_ROWS + 8 + t * BLOCK, 8), BLOCK), :] = tile
            return carry

        lax.fori_loop(0, (n + 7) // 8, some, 0)
    for half in range(2):
        head_copies[half].wait()
        out[half * B_ROWS : half * B_ROWS + 8, :] = headv[half].astype(F32)


def pack_b(rnd, mask_b, b, after):
    smem = pl.BlockSpec(memory_space=pltpu.SMEM)
    vmem = pl.BlockSpec(memory_space=pltpu.VMEM)
    return pl.pallas_call(
        pack_b_kernel,
        in_specs=[smem, smem, pl.BlockSpec(memory_space=pl.ANY), pl.BlockSpec(memory_space=pl.ANY)],
        out_specs=[vmem, smem],
        out_shape=[jax.ShapeDtypeStruct((2 * B_ROWS, 128), F32), jax.ShapeDtypeStruct((1,), I32)],
        scratch_shapes=[
            pltpu.VMEM(b.shape, F32),
            pltpu.SMEM((MESSAGES, 8, 128), I32),
            pltpu.SMEM((MESSAGES, 128), I32),
            pltpu.SMEM((MESSAGES,), I32),
            pltpu.VMEM((2, 8, 128), I32),
            pltpu.SemaphoreType.DMA((6,)),
        ],
        compiler_params=pltpu.CompilerParams(vmem_limit_bytes=8 << 20),
        cost_estimate=_cost(6),
        name="pack_b",
    )(rnd, mask_b, b, after)


def _halves(x):
    hi = x.astype(BF16).astype(F32)
    return hi, x - hi


def unpack_a_kernel(*refs):
    n_a = A_SHARDS // A_PER_GROUP
    a_refs, refs = refs[:n_a], refs[n_a + 1 :]
    lhs, tab, token, ahead, aheadv, sem = refs
    for g in range(n_a):
        for q in range(A_PER_GROUP):
            aheadv[g * A_PER_GROUP + q : g * A_PER_GROUP + q + 1, :] = a_refs[g][q * A_ROWS : q * A_ROWS + 1, :].astype(I32)
    a_head_copy = pltpu.make_async_copy(aheadv, ahead, sem)
    a_head_copy.start()
    a_head_copy.wait()
    low = _lane(BLOCK) < 64
    group = I32(0)
    for g in range(n_a):

        def shard(r, group, g=g):
            q = g * A_PER_GROUP + r
            n0, n1, at = ahead[q, 8], ahead[q, 9], ahead[q, 10]
            g0, g1 = (n0 + 3) >> 2, (n1 + 3) >> 2
            tab[TAB_GROUP + 2 * at] = group
            tab[TAB_GROUP + 2 * at + 1] = group + g0
            tab[TAB_GROUPS + 2 * at] = g0
            tab[TAB_GROUPS + 2 * at + 1] = g1
            for s in range(12):
                tab[TAB_ROW + 4 * group + s] = DUMP
            tiles = []
            for t in range(A_TILES):
                x = a_refs[g][pl.ds(pl.multiple_of(r * A_ROWS + 8 + t * BLOCK, 8), BLOCK), :]
                swapped = pltpu.roll(x, 64, 1)
                for p in range(2):
                    hi, lo = _halves(jnp.where(low, x, swapped) if p == 0 else jnp.where(low, swapped, x))
                    tiles.append(jnp.where(low, hi, lo).astype(BF16))
            for s in range(A_SLOTS):
                place = 4 * group + s + jnp.where(s < n0, 0, 4 * g0 - n0)
                place = jnp.where(s < n0 + n1, place, 4 * GROUPS)
                tab[TAB_ROW + place] = ahead[q, s] * 8
                lhs[pl.ds(pl.multiple_of(place * BLOCK, BLOCK), BLOCK), :] = tiles[s]
            return group + g0 + g1

        group = lax.fori_loop(0, A_PER_GROUP, shard, group)
    for s in range(4):
        tab[TAB_ROW + 4 * GROUPS + s] = DUMP
    token[0] = group


def unpack_a(a_parts, token):
    smem = pl.BlockSpec(memory_space=pltpu.SMEM)
    vmem = pl.BlockSpec(memory_space=pltpu.VMEM)
    return pl.pallas_call(
        unpack_a_kernel,
        in_specs=[vmem] * len(a_parts) + [smem],
        out_specs=[vmem, smem, smem],
        out_shape=[
            jax.ShapeDtypeStruct((4 * (GROUPS + 1) * BLOCK, 128), BF16),
            jax.ShapeDtypeStruct((TAB,), I32),
            jax.ShapeDtypeStruct((1,), I32),
        ],
        scratch_shapes=[pltpu.SMEM((A_SHARDS, 128), I32), pltpu.VMEM((A_SHARDS, 128), I32), pltpu.SemaphoreType.DMA],
        compiler_params=pltpu.CompilerParams(vmem_limit_bytes=16 << 20),
        cost_estimate=_cost(6),
        name="unpack_a",
    )(*a_parts, token)


def product_kernel(*refs, held, first, last):
    n_half = sum(held)
    lhs_hbm, tab, _, refs = refs[0], refs[1], refs[2], refs[3:]
    b_refs, refs = refs[: len(held)], refs[len(held) :]
    b_refs = [ref.at[pl.ds(B_ROWS * q, B_ROWS), :] for ref, n in zip(b_refs, held) for q in range(n)]
    c, refs = refs[0], refs[1:]
    if last:
        c_out, refs = refs[0], refs[1:]
    most_out, bhead, bheadv, rhs, wg, we, wj0, wj1, lhs, sem = refs
    lhs_copy = pltpu.make_async_copy(lhs_hbm, lhs, sem.at[1])
    lhs_copy.start()

    for h in range(n_half):
        bheadv[h] = b_refs[h][0:8, :].astype(I32)
    b_head_copy = pltpu.make_async_copy(bheadv, bhead, sem.at[0])
    b_head_copy.start()
    if first:
        c[...] = jnp.zeros(c.shape, F32)
    b_head_copy.wait()
    most = I32(0)
    work = I32(0)
    for h in range(n_half):
        head, body = bhead.at[h], b_refs[h]
        n = head[H_COUNT, 0]
        most = jnp.maximum(most, head[H_COUNT, 1])

        def unpack(m, w, h=h, head=head, body=body, n=n):
            tiles = []
            for u in range(UNPACK):
                at = jnp.minimum(UNPACK * m + u, n - 1)
                for hl, hr in ((H_L0, H_R0), (H_L1, H_R1)):
                    left, right = head[hl, at], head[hr, at]
                    from_lane = jnp.where(left < 0, 64, 0)
                    to_lane = jnp.where(right < 0, 64, 128)
                    left, right = jnp.maximum(left, 0), jnp.maximum(right, 0)
                    xl = body[pl.ds(pl.multiple_of(8 + (left >> 1) * BLOCK, 8), BLOCK), :]
                    xr = body[pl.ds(pl.multiple_of(8 + (right >> 1) * BLOCK, 8), BLOCK), :]
                    v = _side_by_side(xl, xr, left & 1, right & 1, (from_lane, to_lane))
                    hi, lo = _halves(v)
                    tiles.append((hi.astype(BF16), lo.astype(BF16)))
            for u in range(UNPACK):
                t = UNPACK * m + u
                at = jnp.minimum(t, n - 1)
                place = h * E_STRIDE + t
                for p in range(2):
                    for part in range(2):
                        rhs[pl.ds(pl.multiple_of(place * 256 + p * 128 + part * 64, BLOCK), BLOCK), :] = tiles[2 * u + p][part]
                k, j0, j1 = head[H_K, at], head[H_J0, at], head[H_J1, at]
                group, groups = tab[TAB_GROUP + k], tab[TAB_GROUPS + k]
                groups = jnp.where(t < n, groups, 0)
                for extra in range(2):
                    wg[w] = group + extra
                    we[w] = place
                    wj0[w] = j0
                    wj1[w] = j1
                    w = w + (groups > extra).astype(I32)
            return w

        work = lax.fori_loop(0, (n + UNPACK - 1) // UNPACK, unpack, work)
    for u in range(UNROLL):
        wg[work + u] = GROUPS
        we[work + u] = 0
        wj0[work + u] = 0
        wj1[work + u] = 0

    def multiply(m, carry):
        results = []
        for u in range(UNROLL):
            w = UNROLL * m + u
            left = lhs[pl.ds(pl.multiple_of(wg[w] * 256, 256), 256), :]
            both = rhs[pl.ds(pl.multiple_of(we[w] * 256, 256), 256), :]
            cols = []
            for p in range(2):
                hi, lo = both[p * 128 : p * 128 + 64], both[p * 128 + 64 : p * 128 + 128]
                cols.append(jnp.concatenate([hi, hi, lo, lo], axis=0))
            results.append(
                jnp.dot(
                    jnp.concatenate([left, left], axis=1),
                    jnp.concatenate(cols, axis=1),
                    preferred_element_type=F32,
                )
            )
        for u in range(UNROLL):
            w = UNROLL * m + u
            g = wg[w]
            rows = [tab[TAB_ROW + 4 * g + q] for q in range(4)]
            for p, j in enumerate((wj0[w], wj1[w])):
                sums = [c[rows[q] + j] + results[u][q * BLOCK : (q + 1) * BLOCK, p * 128 : (p + 1) * 128] for q in range(4)]
                for q in range(4):
                    c[rows[q] + j] = sums[q]
        return carry

    lhs_copy.wait()
    lax.fori_loop(0, (work + UNROLL - 1) // UNROLL, multiply, 0)
    most_out[0] = most
    if last:
        out_copies = [
            pltpu.make_async_copy(c.at[8 * i + j], c_out.at[pl.ds(i * BLOCK, BLOCK), pl.ds(j * 128, 128)], sem.at[2])
            for i in range(16)
            for j in range(8)
        ]
        for copy in out_copies:
            copy.start()
        pltpu.make_async_copy(c_out, c_out, sem.at[2]).wait()


def product(lhs, tab, c, halves, first=False, last=False):
    held = [x.shape[0] // B_ROWS for x in halves]
    n_half = sum(held)
    smem = pl.BlockSpec(memory_space=pltpu.SMEM)
    vmem = pl.BlockSpec(memory_space=pltpu.VMEM)
    scratch = [
        pltpu.SMEM((n_half, 8, 128), I32),
        pltpu.VMEM((n_half, 8, 128), I32),
        pltpu.VMEM((n_half * E_STRIDE * 256, 128), BF16),
        pltpu.SMEM((1024,), I32),
        pltpu.SMEM((1024,), I32),
        pltpu.SMEM((1024,), I32),
        pltpu.SMEM((1024,), I32),
        pltpu.VMEM(lhs.shape, BF16),
        pltpu.SemaphoreType.DMA((3,)),
    ]
    out_specs, out_shape = [vmem], [jax.ShapeDtypeStruct((C_TILES, BLOCK, 128), F32)]
    args = (lhs, tab, c) + tuple(halves)
    in_specs = [pl.BlockSpec(memory_space=pltpu.HBM), smem, smem if first else vmem] + [vmem] * len(halves)
    aliases = {} if first else {2: 0}
    if last:
        out_specs.append(pl.BlockSpec(memory_space=pltpu.HBM))
        out_shape.append(jax.ShapeDtypeStruct((1024, 1024), F32))
    out_specs.append(smem)
    out_shape.append(jax.ShapeDtypeStruct((1,), I32))

    def kernel(*refs):
        product_kernel(*refs, held=held, first=first, last=last)

    return pl.pallas_call(
        kernel,
        in_specs=in_specs,
        out_specs=out_specs,
        out_shape=out_shape,
        input_output_aliases=aliases,
        scratch_shapes=scratch,
        compiler_params=pltpu.CompilerParams(vmem_limit_bytes=(n_half * 3 + 14) << 20),
        cost_estimate=_cost(8 if last else 20),
        name="product_first" if first else "product_last" if last else "product_more",
    )(*args)


def _flat(zl, y, zh, core):
    return ((zl * 4 + y) * 2 + zh) * 2 + core


def _turn(step, swapped):
    pairs = []
    for z in range(4):
        for y in range(4):
            for core in range(2):
                along_y = (core == 0) != swapped
                to_y, to_z = ((y + step) % 4, z) if along_y else (y, (z + step) % 4)
                pairs.append((_flat(z % 2, y, z // 2, core), _flat(to_z % 2, to_y, to_z // 2, core)))
    return pairs


def gather_a(packed, token):
    near = [packed] + [lax.ppermute(packed, AXES, _turn(s, False)) for s in (1, 3, 2)]
    *near, token = lax.optimization_barrier((*near, token))
    group = jnp.concatenate(near, axis=0)
    mine = [group] + [lax.ppermute(group, AXES, _turn(s, True)) for s in (1, 3, 2)]
    late = lax.optimization_barrier((group, mine[1], mine[2]))[0]
    other = [lax.ppermute(x, "core", [(0, 1), (1, 0)]) for x in mine[1:] + [late]]
    return mine + other, token


UP = [(i, (i + 1) % ROWS) for i in range(ROWS)]
DOWN = [(i, (i - 1) % ROWS) for i in range(ROWS)]


def near_b(p):
    return lax.ppermute(p, "row", UP), lax.ppermute(p, "row", DOWN)


def far_b(above, below):
    return lax.ppermute(above[:B_ROWS], "row", UP), lax.ppermute(below[B_ROWS:], "row", DOWN)


def shards(a_blocks, mask_a, b_blocks, mask_b):
    pa = pack_a(mask_a, a_blocks)
    p, token = pack_b(jnp.zeros((1,), I32), mask_b, b_blocks, pa)
    near = near_b(p)
    a_parts, token = gather_a(pa, token)
    lhs, tab, token = unpack_a(a_parts, token)
    *near, token = lax.optimization_barrier((*near, token))
    far = far_b(*near)
    c, most0 = product(lhs, tab, token, (p, *near), first=True)
    _, out, most1 = product(lhs, tab, c, far, last=True)
    most = jnp.maximum(most0, most1)[0]

    def again(carry):
        r, out = carry
        p, _ = pack_b(r[None], mask_b, b_blocks, pa)
        near = near_b(p)
        far = far_b(*near)
        c = out.reshape(16, BLOCK, 8, 128).transpose(0, 2, 1, 3).reshape(128, BLOCK, 128)
        c = jnp.pad(c, ((0, C_TILES - 128), (0, 0), (0, 0)))
        c, _ = product(lhs, tab, c, (p,) + near[:1])
        return r + 1, product(lhs, tab, c, near[1:] + far, last=True)[1]

    return lax.while_loop(lambda carry: carry[0] * 2 < most, again, (I32(1), out))[1]


def solution(mesh):
    fine = Mesh(mesh.devices.reshape(4, 2, 4, 2, 2), ("row",) + AXES)
    placed = P("row", AXES)
    return jax.shard_map(shards, mesh=fine, in_specs=(placed,) * 4, out_specs=placed, check_vma=False)
```

time: 393 us -> 74.7 us (0.19)
  waiting for transfers between devices: 255 us -> 18.9 us
  matrix products: 110 us -> 0 us
  Pallas kernels: 0 us -> 33.6 us
  starting transfers between devices: 0.04 us -> 16.4 us
  between operations: 13.4 us -> 1.61 us
  other arithmetic: 6.62 us -> 0 us
    all_gather x2 -> x0, waiting for transfers between devices: 255 us -> none  [the longest x1 155 us: shards(): b_whole = lax.all_gather(b_masked, 'row', axis=0, tiled=True)]
    dot_general x1 -> x0, matrix products: 110 us -> none  [shards(): jnp.dot(lax.all_gather(a_masked, ('col', 'layer'), axis=1, tiled=True), b...]
    pallas_call x0 -> x5, Pallas kernels: none -> 33.6 us  [the longest x2 19 us: product(): pl.pallas_call(kernel, in_specs=in_specs, out_specs=out_specs, out_shape=...]
    ppermute x0 -> x14, waiting for transfers between devices: none -> 18.9 us  [the longest x3 9.39 us: gather_a(): lax.ppermute(group, AXES, _turn(s, True))]
    ppermute x0 -> x14, starting transfers between devices: none -> 16.4 us  [the longest x3 5.98 us: gather_a(): lax.ppermute(group, AXES, _turn(s, True))]
    mul x2 -> x0, other arithmetic: 5.92 us -> none  [the longest x1 5.06 us: shards(): b_masked = b_blocks * expand(mask_b)]
    unnamed x6 -> x11, local copies, waits for them, and re-layouts: 5.6 us -> 1.34 us
  transfers between devices with their start and end apart: 2 -> 14, of which waited for: 2 -> 7; matrix products, arithmetic and copies ran while one was open for 0% -> 0% of each run, Pallas kernels for 0% -> 34%
where the time goes in v2:
time: 74.7 us; the launch traced here: 73.9 us
  Pallas kernels  33.6 us (45%)
  waiting for transfers between devices  18.9 us (25%)
  starting transfers between devices  16.4 us (22%)
  local copies, waits for them, and re-layouts  3.17 us (4%)
  between operations  1.61 us (2%)
    pallas_call x2, Pallas kernels, product(): pl.pallas_call(kernel, in_specs=in_specs, out_specs=out_specs, out_shape=...  19 us
    ppermute x3, waiting for transfers between devices, gather_a(): lax.ppermute(group, AXES, _turn(s, True))  9.39 us
    pallas_call x1, Pallas kernels, unpack_a(): pl.pallas_call(unpack_a_kernel, in_specs=[vmem] * len(a_parts) + [smem],...  7.91 us
    ppermute x2, waiting for transfers between devices, near_b(): return (lax.ppermute(p, 'row', UP), lax.ppermute(p, 'row', DOWN))  6.18 us
    ppermute x3, starting transfers between devices, gather_a(): lax.ppermute(group, AXES, _turn(s, True))  5.98 us
    pallas_call x1, Pallas kernels, pack_b(): pl.pallas_call(pack_b_kernel, in_specs=[smem, smem, pl.BlockSpec(memory_s...  5.42 us
    ppermute x3, starting transfers between devices, gather_a(): lax.ppermute(packed, AXES, _turn(s, False))  5.38 us
    ppermute x4, waiting for transfers between devices, gather_a(): lax.ppermute(x, 'core', [(0, 1), (1, 0)])  2.96 us
  transfers between devices with their start and end apart: 14, of which 7 were waited for; matrix products, arithmetic and copies ran while one was open for 0% of the time, Pallas kernels for 34%

profile of v2, /device:TPU:0, one launch (start us, length us, event | category | flops | bytes accessed | tf_op | source)
XLA Modules:
  0.0 73.9 jit_solution(15348282536639061515)
XLA Ops:
  0.0 1.2 %pack_a.1.after_ref = f32[264,128]{1,0:T(8,128)S(1)} custom-call(s32[2,16]{1,0:T(2,128)} %bitcast.22, f32[1024,128]{1,0:T(8,128)} %a_ref.1), custom_call_target="tpu_custom_call" | custom-call | bytes 7380000 | tf_op jit(solution)/shard_map/pack_a/pallas_call | solution.py:75
  1.2 3.4 %collective-permute-start.6 = (f32[264,128]{1,0:T(8,128)S(1)}, f32[264,128]{1,0:T(8,128)S(1)}, u32[]{:S(2)}, u32[]{:S(2)}) collective-permute-start(f32[264,128]{1,0:T(8,128)S(1)} %pack_a.1.after_ref), channel_id=1, source_target_pairs={{0,8},{1,3},{4,12},{5,7},{8,0},{9,11},{12,4},{13,15},{16,24},{17,1... | collective-permute-start | bytes 405512 | tf_op jit(solution)/shard_map/ppermute | solution.py:413
  4.6 1.1 %collective-permute-start.5 = (f32[264,128]{1,0:T(8,128)S(1)}, f32[264,128]{1,0:T(8,128)S(1)}, u32[]{:S(2)}, u32[]{:S(2)}) collective-permute-start(f32[264,128]{1,0:T(8,128)S(1)} %pack_a.1.after_ref), channel_id=1, source_target_pairs={{0,12},{1,19},{4,0},{5,23},{8,4},{9,27},{12,8},{13,31},{16,28},{17... | collective-permute-start | bytes 405512 | tf_op jit(solution)/shard_map/ppermute | solution.py:413
  5.6 1.0 %collective-permute-start.4 = (f32[264,128]{1,0:T(8,128)S(1)}, f32[264,128]{1,0:T(8,128)S(1)}, u32[]{:S(2)}, u32[]{:S(2)}) collective-permute-start(f32[264,128]{1,0:T(8,128)S(1)} %pack_a.1.after_ref), channel_id=1, source_target_pairs={{0,4},{1,17},{4,8},{5,21},{8,12},{9,25},{12,0},{13,29},{16,20},{17... | collective-permute-start | bytes 405512 | tf_op jit(solution)/shard_map/ppermute | solution.py:413
  6.6 5.4 %pack_b.5 = (f32[2448,128]{1,0:T(8,128)S(1)}, s32[1]{0:T(128)}) custom-call(s32[1]{0:T(128)} %constant.18.clone.1.round_ref, s32[16,16]{1,0:T(8,128)} %mask_ref.1, f32[1024,1024]{1,0:T(8,128)} %b_hbm.1, f32[264,128]{1,0:T(8,128)S(1)} %pack_a.1.after_ref), custom_call_target="tpu_custom_call" | custom-call | bytes 22140000 | tf_op jit(solution)/shard_map/pack_b/pallas_call | solution.py:162
  12.0 0.0 copy-start.2
  12.0 0.0 collective-permute-done.6
  12.0 0.0 collective-permute-done.4
  12.1 4.0 %collective-permute-start.9 = (f32[1056,128]{1,0:T(8,128)S(1)}, f32[1056,128]{1,0:T(8,128)S(1)}, u32[]{:S(2)}, u32[]{:S(2)}) collective-permute-start(f32[1056,128]{1,0:T(8,128)S(1)} %constant_dynamic-update-slice_fusion.refs_0_), channel_id=1, source_target_pairs={{0,2},{1,9},{4,6},{5,13},{8,10},{9,1},{12,14},{13,5},{16,18},{17,2... | collective-permute-start | bytes 1622024 | tf_op jit(solution)/shard_map/ppermute | solution.py:416
  16.1 2.5 %collective-permute-start.15 = (f32[2448,128]{1,0:T(8,128)S(1)}, f32[2448,128]{1,0:T(8,128)S(1)}, u32[]{:S(2)}, u32[]{:S(2)}) collective-permute-start(f32[2448,128]{1,0:T(8,128)S(1)} %get-tuple-element.136.refs_3_), channel_id=1, source_target_pairs={{0,96},{32,0},{64,32},{96,64},{1,97},{33,1},{65,33},{97,65},{2,98}... | collective-permute-start | bytes 3760136 | tf_op jit(solution)/shard_map/ppermute | solution.py:427
  18.6 0.0 collective-permute-start.14
  18.6 0.7 collective-permute-start.8
  19.3 1.3 %collective-permute-start.7 = (f32[1056,128]{1,0:T(8,128)S(1)}, f32[1056,128]{1,0:T(8,128)S(1)}, u32[]{:S(2)}, u32[]{:S(2)}) collective-permute-start(f32[1056,128]{1,0:T(8,128)S(1)} %constant_dynamic-update-slice_fusion.refs_0_), channel_id=1, source_target_pairs={{0,16},{1,5},{4,20},{5,9},{8,24},{9,13},{12,28},{13,1},{16,2},{17,... | collective-permute-start | bytes 1622024 | tf_op jit(solution)/shard_map/ppermute | solution.py:416
  20.7 2.8 %collective-permute-done.9.refs_3_ = f32[1056,128]{1,0:T(8,128)S(1)} collective-permute-done((f32[1056,128]{1,0:T(8,128)S(1)}, f32[1056,128]{1,0:T(8,128)S(1)}, u32[]{:S(2)}, u32[]{:S(2)}) %collective-permute-start.9) | collective-permute-done | bytes 540704 | tf_op jit(solution)/shard_map/ppermute | solution.py:416
  23.4 0.0 collective-permute-start.12
  23.4 6.6 %collective-permute-done.8.refs_2_ = f32[1056,128]{1,0:T(8,128)S(1)} collective-permute-done((f32[1056,128]{1,0:T(8,128)S(1)}, f32[1056,128]{1,0:T(8,128)S(1)}, u32[]{:S(2)}, u32[]{:S(2)}) %collective-permute-start.8) | collective-permute-done | bytes 540704 | tf_op jit(solution)/shard_map/ppermute | solution.py:416
  30.1 0.5 collective-permute-start.11
  30.6 0.0 collective-permute-start.10
  30.6 2.2 %collective-permute-done.11.refs_5_ = f32[1056,128]{1,0:T(8,128)S(1)} collective-permute-done((f32[1056,128]{1,0:T(8,128)S(1)}, f32[1056,128]{1,0:T(8,128)S(1)}, u32[]{:S(2)}, u32[]{:S(2)}) %collective-permute-start.11) | collective-permute-done | bytes 540704 | tf_op jit(solution)/shard_map/ppermute | solution.py:418
  32.8 0.8 %collective-permute-done.10.refs_4_ = f32[1056,128]{1,0:T(8,128)S(1)} collective-permute-done((f32[1056,128]{1,0:T(8,128)S(1)}, f32[1056,128]{1,0:T(8,128)S(1)}, u32[]{:S(2)}, u32[]{:S(2)}) %collective-permute-start.10) | collective-permute-done | bytes 540704 | tf_op jit(solution)/shard_map/ppermute | solution.py:418
  33.5 7.9 %unpack_a.1 = (bf16[24832,128]{1,0:T(8,128)(2,1)}, s32[1024]{0:T(1024)S(1)}, s32[1]{0:T(128)}) custom-call(f32[1056,128]{1,0:T(8,128)S(1)} %constant_dynamic-update-slice_fusion.refs_0_, f32[1056,128]{1,0:T(8,128)S(1)} %collective-permute-done.7.refs_1_, f32[1056,128]{1,0:T(8,128)S(1)} %collective-permute-done.8.refs_2_, ...), custom_call_target="tpu_custom_call" | custom-call | bytes 22140000 | tf_op jit(solution)/shard_map/unpack_a/pallas_call | solution.py:233
  41.5 2.8 %collective-permute-done.15.refs_5_ = f32[2448,128]{1,0:T(8,128)S(1)} collective-permute-done((f32[2448,128]{1,0:T(8,128)S(1)}, f32[2448,128]{1,0:T(8,128)S(1)}, u32[]{:S(2)}, u32[]{:S(2)}) %collective-permute-start.15) | collective-permute-done | bytes 1253408 | tf_op jit(solution)/shard_map/ppermute | solution.py:427
  44.2 3.4 %collective-permute-done.14.refs_4_ = f32[2448,128]{1,0:T(8,128)S(1)} collective-permute-done((f32[2448,128]{1,0:T(8,128)S(1)}, f32[2448,128]{1,0:T(8,128)S(1)}, u32[]{:S(2)}, u32[]{:S(2)}) %collective-permute-start.14) | collective-permute-done | bytes 1253408 | tf_op jit(solution)/shard_map/ppermute | solution.py:427
  47.6 0.9 %slice.18 = f32[1224,128]{1,0:T(8,128)} slice(f32[2448,128]{1,0:T(8,128)S(1)} %collective-permute-done.14.refs_4_), slice={[0:1224], [0:128]} | slice | bytes 1253376 | tf_op jit(solution)/shard_map/slice | solution.py:431
  48.5 0.9 %slice.19 = f32[1224,128]{1,0:T(8,128)} slice(f32[2448,128]{1,0:T(8,128)S(1)} %collective-permute-done.15.refs_5_), slice={[1224:2448], [0:128]} | slice | bytes 1253376 | tf_op jit(solution)/shard_map/slice | solution.py:431
  49.5 0.3 collective-permute-start.17
  49.7 1.7 %collective-permute-start.16 = (f32[1224,128]{1,0:T(8,128)}, f32[1224,128]{1,0:T(8,128)}, u32[]{:S(2)}, u32[]{:S(2)}) collective-permute-start(f32[1224,128]{1,0:T(8,128)} %slice.18), channel_id=1, source_target_pairs={{0,32},{32,64},{64,96},{96,0},{1,33},{33,65},{65,97},{97,1},{2,34}... | collective-permute-start | bytes 1880072 | tf_op jit(solution)/shard_map/ppermute | solution.py:431
  51.5 1.3 %copy-done.3 = f32[2448,128]{1,0:T(8,128)S(1)} copy-done((f32[2448,128]{1,0:T(8,128)S(1)}, f32[2448,128]{1,0:T(8,128)}, u32[]{:S(2)}) %copy-start.3) | copy-done | bytes 1253400
  52.8 11.5 %product_first.1 = (f32[136,64,128]{2,1,0:T(8,128)S(1)}, s32[1]{0:T(128)}) custom-call(bf16[24832,128]{1,0:T(8,128)(2,1)} %get-tuple-element.224.refs_0_, s32[1024]{0:T(1024)S(1)} %get-tuple-element.225.refs_1_, s32[1]{0:T(128)} %get-tuple-element.138.refs_2_, f32[2448,128]{1,0:T(8,128)S(1)} %copy-done.3, f32[2448,128]{1,0:T(8,128)S(1)} %collective-permute-done.14.refs_4_, ...), custom_call_target="tpu_custom_call" | custom-call | bytes 73800000 | tf_op jit(solution)/shard_map/product_first/pallas_call | solution.py:384
  64.3 0.4 collective-permute-done.16.refs_3_
  64.7 7.5 %product_last.5 = (f32[136,64,128]{2,1,0:T(8,128)S(1)}, f32[1024,1024]{1,0:T(8,128)}, s32[1]{0:T(128)}) custom-call(bf16[24832,128]{1,0:T(8,128)(2,1)S(1)} %copy-done.4, s32[1024]{0:T(1024)S(1)} %get-tuple-element.225.refs_1_, f32[136,64,128]{2,1,0:T(8,128)S(1)} %get-tuple-element.141.refs_2_, ...), custom_call_target="tpu_custom_call", output_to_operand_aliasing={{0}: (2, {})} | custom-call | bytes 29520000 | tf_op jit(solution)/shard_map/product_last/pallas_call | solution.py:384
  73.6 0.2 while.12
  (16 shorter events, 0.1 us)
Async XLA Ops:
  1.2 10.8 %collective-permute-start.6 = (f32[264,128]{1,0:T(8,128)S(1)}, f32[264,128]{1,0:T(8,128)S(1)}, u32[]{:S(2)}, u32[]{:S(2)}) collective-permute-start(f32[264,128]{1,0:T(8,128)S(1)} %pack_a.1.after_ref), channel_id=1, source_target_pairs={{0,8},{1,3},{4,12},{5,7},{8,0},{9,11},{12,4},{13,15},{16,24},{17,1... | collective-permute-start | bytes 405512 | tf_op jit(solution)/shard_map/ppermute | solution.py:413
  4.6 7.5 %collective-permute-start.5 = (f32[264,128]{1,0:T(8,128)S(1)}, f32[264,128]{1,0:T(8,128)S(1)}, u32[]{:S(2)}, u32[]{:S(2)}) collective-permute-start(f32[264,128]{1,0:T(8,128)S(1)} %pack_a.1.after_ref), channel_id=1, source_target_pairs={{0,12},{1,19},{4,0},{5,23},{8,4},{9,27},{12,8},{13,31},{16,28},{17... | collective-permute-start | bytes 405512 | tf_op jit(solution)/shard_map/ppermute | solution.py:413
  5.6 6.4 %collective-permute-start.4 = (f32[264,128]{1,0:T(8,128)S(1)}, f32[264,128]{1,0:T(8,128)S(1)}, u32[]{:S(2)}, u32[]{:S(2)}) collective-permute-start(f32[264,128]{1,0:T(8,128)S(1)} %pack_a.1.after_ref), channel_id=1, source_target_pairs={{0,4},{1,17},{4,8},{5,21},{8,12},{9,25},{12,0},{13,29},{16,20},{17... | collective-permute-start | bytes 405512 | tf_op jit(solution)/shard_map/ppermute | solution.py:413
  12.0 35.6 %copy-start.2 = (f32[2448,128]{1,0:T(8,128)}, f32[2448,128]{1,0:T(8,128)S(1)}, u32[]{:S(2)}) copy-start(f32[2448,128]{1,0:T(8,128)S(1)} %get-tuple-element.136.refs_3_) | copy-start | bytes 3760132
  12.1 11.3 %collective-permute-start.9 = (f32[1056,128]{1,0:T(8,128)S(1)}, f32[1056,128]{1,0:T(8,128)S(1)}, u32[]{:S(2)}, u32[]{:S(2)}) collective-permute-start(f32[1056,128]{1,0:T(8,128)S(1)} %constant_dynamic-update-slice_fusion.refs_0_), channel_id=1, source_target_pairs={{0,2},{1,9},{4,6},{5,13},{8,10},{9,1},{12,14},{13,5},{16,18},{17,2... | collective-permute-start | bytes 1622024 | tf_op jit(solution)/shard_map/ppermute | solution.py:416
  16.1 28.1 %collective-permute-start.15 = (f32[2448,128]{1,0:T(8,128)S(1)}, f32[2448,128]{1,0:T(8,128)S(1)}, u32[]{:S(2)}, u32[]{:S(2)}) collective-permute-start(f32[2448,128]{1,0:T(8,128)S(1)} %get-tuple-element.136.refs_3_), channel_id=1, source_target_pairs={{0,96},{32,0},{64,32},{96,64},{1,97},{33,1},{65,33},{97,65},{2,98}... | collective-permute-start | bytes 3760136 | tf_op jit(solution)/shard_map/ppermute | solution.py:427
  18.6 29.0 %collective-permute-start.14 = (f32[2448,128]{1,0:T(8,128)S(1)}, f32[2448,128]{1,0:T(8,128)S(1)}, u32[]{:S(2)}, u32[]{:S(2)}) collective-permute-start(f32[2448,128]{1,0:T(8,128)S(1)} %get-tuple-element.136.refs_3_), channel_id=1, source_target_pairs={{0,32},{32,64},{64,96},{96,0},{1,33},{33,65},{65,97},{97,1},{2,34}... | collective-permute-start | bytes 3760136 | tf_op jit(solution)/shard_map/ppermute | solution.py:427
  18.6 11.4 %collective-permute-start.8 = (f32[1056,128]{1,0:T(8,128)S(1)}, f32[1056,128]{1,0:T(8,128)S(1)}, u32[]{:S(2)}, u32[]{:S(2)}) collective-permute-start(f32[1056,128]{1,0:T(8,128)S(1)} %constant_dynamic-update-slice_fusion.refs_0_), channel_id=1, source_target_pairs={{0,18},{1,13},{4,22},{5,1},{8,26},{9,5},{12,30},{13,9},{16,0},{17,... | collective-permute-start | bytes 1622024 | tf_op jit(solution)/shard_map/ppermute | solution.py:416
  19.3 10.7 %collective-permute-start.7 = (f32[1056,128]{1,0:T(8,128)S(1)}, f32[1056,128]{1,0:T(8,128)S(1)}, u32[]{:S(2)}, u32[]{:S(2)}) collective-permute-start(f32[1056,128]{1,0:T(8,128)S(1)} %constant_dynamic-update-slice_fusion.refs_0_), channel_id=1, source_target_pairs={{0,16},{1,5},{4,20},{5,9},{8,24},{9,13},{12,28},{13,1},{16,2},{17,... | collective-permute-start | bytes 1622024 | tf_op jit(solution)/shard_map/ppermute | solution.py:416
  23.4 7.1 %collective-permute-start.12 = (f32[1056,128]{1,0:T(8,128)S(1)}, f32[1056,128]{1,0:T(8,128)S(1)}, u32[]{:S(2)}, u32[]{:S(2)}) collective-permute-start(f32[1056,128]{1,0:T(8,128)S(1)} %collective-permute-done.9.refs_3_), channel_id=1, source_target_pairs={{0,1},{1,0},{2,3},{3,2},{4,5},{5,4},{6,7},{7,6},{8,9},{9,8},{10,11... | collective-permute-start | bytes 1622024 | tf_op jit(solution)/shard_map/ppermute | solution.py:418
  30.1 2.7 %collective-permute-start.13 = (f32[1056,128]{1,0:T(8,128)S(1)}, f32[1056,128]{1,0:T(8,128)S(1)}, u32[]{:S(2)}, u32[]{:S(2)}) collective-permute-start(f32[1056,128]{1,0:T(8,128)S(1)} %constant_dynamic-update-slice_fusion.refs_0_), channel_id=1, source_target_pairs={{0,1},{1,0},{2,3},{3,2},{4,5},{5,4},{6,7},{7,6},{8,9},{9,8},{10,11... | collective-permute-start | bytes 1622024 | tf_op jit(solution)/shard_map/ppermute | solution.py:418
  30.1 2.7 %collective-permute-start.11 = (f32[1056,128]{1,0:T(8,128)S(1)}, f32[1056,128]{1,0:T(8,128)S(1)}, u32[]{:S(2)}, u32[]{:S(2)}) collective-permute-start(f32[1056,128]{1,0:T(8,128)S(1)} %collective-permute-done.8.refs_2_), channel_id=1, source_target_pairs={{0,1},{1,0},{2,3},{3,2},{4,5},{5,4},{6,7},{7,6},{8,9},{9,8},{10,11... | collective-permute-start | bytes 1622024 | tf_op jit(solution)/shard_map/ppermute | solution.py:418
  30.6 3.0 %collective-permute-start.10 = (f32[1056,128]{1,0:T(8,128)S(1)}, f32[1056,128]{1,0:T(8,128)S(1)}, u32[]{:S(2)}, u32[]{:S(2)}) collective-permute-start(f32[1056,128]{1,0:T(8,128)S(1)} %collective-permute-done.7.refs_1_), channel_id=1, source_target_pairs={{0,1},{1,0},{2,3},{3,2},{4,5},{5,4},{6,7},{7,6},{8,9},{9,8},{10,11... | collective-permute-start | bytes 1622024 | tf_op jit(solution)/shard_map/ppermute | solution.py:418
  49.5 14.9 %collective-permute-start.17 = (f32[1224,128]{1,0:T(8,128)}, f32[1224,128]{1,0:T(8,128)S(1)}, u32[]{:S(2)}, u32[]{:S(2)}) collective-permute-start(f32[1224,128]{1,0:T(8,128)} %slice.19), channel_id=1, source_target_pairs={{0,96},{32,0},{64,32},{96,64},{1,97},{33,1},{65,33},{97,65},{2,98}... | collective-permute-start | bytes 1880072 | tf_op jit(solution)/shard_map/ppermute | solution.py:431
  49.7 15.0 %collective-permute-start.16 = (f32[1224,128]{1,0:T(8,128)}, f32[1224,128]{1,0:T(8,128)}, u32[]{:S(2)}, u32[]{:S(2)}) collective-permute-start(f32[1224,128]{1,0:T(8,128)} %slice.18), channel_id=1, source_target_pairs={{0,32},{32,64},{64,96},{96,0},{1,33},{33,65},{65,97},{97,1},{2,34}... | collective-permute-start | bytes 1880072 | tf_op jit(solution)/shard_map/ppermute | solution.py:431
  51.5 1.3 %copy-start.3 = (f32[2448,128]{1,0:T(8,128)S(1)}, f32[2448,128]{1,0:T(8,128)}, u32[]{:S(2)}) copy-start(f32[2448,128]{1,0:T(8,128)} %copy-done.2) | copy-start | bytes 3760132
  52.8 11.9 %copy-start.4 = (bf16[24832,128]{1,0:T(8,128)(2,1)S(1)}, bf16[24832,128]{1,0:T(8,128)(2,1)}, u32[]{:S(2)}) copy-start(bf16[24832,128]{1,0:T(8,128)(2,1)} %get-tuple-element.224.refs_0_) | copy-start | bytes 19070980
  64.7 8.8 %copy-start.5 = (s32[16,16]{1,0:T(8,128)S(1)}, s32[16,16]{1,0:T(8,128)}, u32[]{:S(2)}) copy-start(s32[16,16]{1,0:T(8,128)} %mask_ref.1) | copy-start | bytes 3076

commit v3 on v2

--- a/solution.py
+++ b/solution.py
@@ -95,33 +95,44 @@
         heads[m, H_COUNT, 0] = 0
 
     def scan_row(k, carry):
-        m, e, n = carry
-        par = I32(0)
-        for j in range(8):
-            m0, m1 = mask_ref[k, 2 * j], mask_ref[k, 2 * j + 1]
-            count = m0 + m1
-            full = n + count > B_SLOTS
-            m = m + full.astype(I32)
-            e = jnp.where(full, 0, e)
-            n = jnp.where(full, 0, n)
-            par = jnp.where(full, 0, par)
-            at = e - par
-            heads[m, H_K, at] = row * 16 + k
-            heads[m, H_J0 + par, at] = j
-            heads[m, H_J1, at] = j
-            heads[m, H_L1, at] = -1
-            heads[m, H_R1, at] = -1
-            heads[m, H_L0 + 2 * par, at] = jnp.where(m0 == 1, n, -1)
-            heads[m, H_R0 + 2 * par, at] = jnp.where(m1 == 1, n + m0, -1)
-            source[m, n] = k * 16 + 2 * j
-            source[m, n + m0] = k * 16 + 2 * j + 1
-            some = jnp.minimum(count, 1)
-            n = n + count
-            e = e + some * (1 - par)
-            par = par ^ some
+        mask = [mask_ref[k, j] for j in range(16)]
+        total = mask
+        while len(total) > 1:
+            total = [x + y for x, y in zip(total[::2], total[1::2])]
+
+        def scan(carry, may_split):
+            m, e, n = carry
+            par = I32(0)
+            for j in range(8):
+                m0, m1 = mask[2 * j], mask[2 * j + 1]
+                count = m0 + m1
+                if may_split:
+                    full = n + count > B_SLOTS
+                    size[m] = n
+                    heads[m, H_COUNT, 0] = e
+                    m = m + full.astype(I32)
+                    e = jnp.where(full, 0, e)
+                    n = jnp.where(full, 0, n)
+                    par = jnp.where(full, 0, par)
+                some = m0 | m1
+                at = e - par
+                heads[m, H_K, at] = row * 16 + k
+                heads[m, H_J0 + par, at] = j
+                heads[m, H_J1, at] = j
+                heads[m, H_L1, at] = -1
+                heads[m, H_R1, at] = -1
+                heads[m, H_L0 + 2 * par, at] = jnp.where(m0 == 1, n, -1)
+                heads[m, H_R0 + 2 * par, at] = jnp.where(m1 == 1, n + m0, -1)
+                source[m, n] = k * 16 + 2 * j
+                source[m, n + m0] = k * 16 + 2 * j + 1
+                n = n + count
+                par = par ^ some
+                e = at + (par | some)
             size[m] = n
             heads[m, H_COUNT, 0] = e
-        return m, e, n
+            return m, e, n
+
+        return lax.cond(carry[2] + total[0] > B_SLOTS, lambda c: scan(c, True), lambda c: scan(c, False), carry)
 
     last, _, _ = lax.fori_loop(0, 16, scan_row, (I32(0), I32(0), I32(0)))
     token[0] = last
@@ -248,15 +259,19 @@
 
 def product_kernel(*refs, held, first, last):
     n_half = sum(held)
-    lhs_hbm, tab, _, refs = refs[0], refs[1], refs[2], refs[3:]
+    lhs_in, tab, _, refs = refs[0], refs[1], refs[2], refs[3:]
     b_refs, refs = refs[: len(held)], refs[len(held) :]
     b_refs = [ref.at[pl.ds(B_ROWS * q, B_ROWS), :] for ref, n in zip(b_refs, held) for q in range(n)]
     c, refs = refs[0], refs[1:]
     if last:
         c_out, refs = refs[0], refs[1:]
-    most_out, bhead, bheadv, rhs, wg, we, wj0, wj1, lhs, sem = refs
-    lhs_copy = pltpu.make_async_copy(lhs_hbm, lhs, sem.at[1])
-    lhs_copy.start()
+    if last:
+        most_out, bhead, bheadv, rhs, wg, we, wj0, wj1, sem = refs
+        lhs = lhs_in
+    else:
+        most_out, bhead, bheadv, rhs, wg, we, wj0, wj1, lhs, sem = refs
+        lhs_copy = pltpu.make_async_copy(lhs_in, lhs, sem.at[1])
+        lhs_copy.start()
 
     for h in range(n_half):
         bheadv[h] = b_refs[h][0:8, :].astype(I32)
@@ -338,7 +353,8 @@
                     c[rows[q] + j] = sums[q]
         return carry
 
-    lhs_copy.wait()
+    if not last:
+        lhs_copy.wait()
     lax.fori_loop(0, (work + UNROLL - 1) // UNROLL, multiply, 0)
     most_out[0] = most
     if last:
@@ -365,12 +381,12 @@
         pltpu.SMEM((1024,), I32),
         pltpu.SMEM((1024,), I32),
         pltpu.SMEM((1024,), I32),
-        pltpu.VMEM(lhs.shape, BF16),
+        *([] if last else [pltpu.VMEM(lhs.shape, BF16)]),
         pltpu.SemaphoreType.DMA((3,)),
     ]
     out_specs, out_shape = [vmem], [jax.ShapeDtypeStruct((C_TILES, BLOCK, 128), F32)]
     args = (lhs, tab, c) + tuple(halves)
-    in_specs = [pl.BlockSpec(memory_space=pltpu.HBM), smem, smem if first else vmem] + [vmem] * len(halves)
+    in_specs = [vmem if last else pl.BlockSpec(memory_space=pltpu.HBM), smem, smem if first else vmem] + [vmem] * len(halves)
     aliases = {} if first else {2: 0}
     if last:
         out_specs.append(pl.BlockSpec(memory_space=pltpu.HBM))

time: 74.7 us -> 73.3 us (0.981)
  Pallas kernels: 33.6 us -> 32.1 us
    pallas_call x2, Pallas kernels: 19 us -> 17.9 us  [product(): pl.pallas_call(kernel, in_specs=in_specs, out_specs=out_specs, out_shape=...]
  transfers between devices with their start and end apart: 14 -> 14, of which waited for: 7 -> 8; matrix products, arithmetic and copies ran while one was open for 0% -> 0% of each run, Pallas kernels for 34% -> 34%
where the time goes in v3:
time: 73.3 us; the launch traced here: 72.3 us
  Pallas kernels  32.1 us (44%)
  waiting for transfers between devices  18.6 us (25%)
  starting transfers between devices  16.7 us (23%)
  local copies, waits for them, and re-layouts  3.17 us (4%)
  between operations  1.6 us (2%)
    pallas_call x2, Pallas kernels, product(): pl.pallas_call(kernel, in_specs=in_specs, out_specs=out_specs, out_shape=...  17.9 us
    ppermute x3, waiting for transfers between devices, gather_a(): lax.ppermute(group, AXES, _turn(s, True))  9.39 us
    pallas_call x1, Pallas kernels, unpack_a(): pl.pallas_call(unpack_a_kernel, in_specs=[vmem] * len(a_parts) + [smem],...  7.91 us
    ppermute x3, starting transfers between devices, gather_a(): lax.ppermute(group, AXES, _turn(s, True))  5.98 us
    ppermute x2, waiting for transfers between devices, near_b(): return (lax.ppermute(p, 'row', UP), lax.ppermute(p, 'row', DOWN))  5.86 us
    ppermute x3, starting transfers between devices, gather_a(): lax.ppermute(packed, AXES, _turn(s, False))  5.38 us
    pallas_call x1, Pallas kernels, pack_b(): pl.pallas_call(pack_b_kernel, in_specs=[smem, smem, pl.BlockSpec(memory_s...  5.13 us
    ppermute x4, waiting for transfers between devices, gather_a(): lax.ppermute(x, 'core', [(0, 1), (1, 0)])  2.96 us
  transfers between devices with their start and end apart: 14, of which 8 were waited for; matrix products, arithmetic and copies ran while one was open for 0% of the time, Pallas kernels for 34%

profile of v3, /device:TPU:0, one launch (start us, length us, event | category | flops | bytes accessed | tf_op | source)
XLA Modules:
  0.0 72.3 jit_solution(310421944051801191)
XLA Ops:
  0.0 1.2 %pack_a.1.after_ref = f32[264,128]{1,0:T(8,128)S(1)} custom-call(s32[2,16]{1,0:T(2,128)} %bitcast.22, f32[1024,128]{1,0:T(8,128)} %a_ref.1), custom_call_target="tpu_custom_call" | custom-call | bytes 7380000 | tf_op jit(solution)/shard_map/pack_a/pallas_call | solution.py:75
  1.2 3.4 %collective-permute-start.6 = (f32[264,128]{1,0:T(8,128)S(1)}, f32[264,128]{1,0:T(8,128)S(1)}, u32[]{:S(2)}, u32[]{:S(2)}) collective-permute-start(f32[264,128]{1,0:T(8,128)S(1)} %pack_a.1.after_ref), channel_id=1, source_target_pairs={{0,8},{1,3},{4,12},{5,7},{8,0},{9,11},{12,4},{13,15},{16,24},{17,1... | collective-permute-start | bytes 405512 | tf_op jit(solution)/shard_map/ppermute | solution.py:429
  4.6 1.1 %collective-permute-start.5 = (f32[264,128]{1,0:T(8,128)S(1)}, f32[264,128]{1,0:T(8,128)S(1)}, u32[]{:S(2)}, u32[]{:S(2)}) collective-permute-start(f32[264,128]{1,0:T(8,128)S(1)} %pack_a.1.after_ref), channel_id=1, source_target_pairs={{0,12},{1,19},{4,0},{5,23},{8,4},{9,27},{12,8},{13,31},{16,28},{17... | collective-permute-start | bytes 405512 | tf_op jit(solution)/shard_map/ppermute | solution.py:429
  5.6 1.0 %collective-permute-start.4 = (f32[264,128]{1,0:T(8,128)S(1)}, f32[264,128]{1,0:T(8,128)S(1)}, u32[]{:S(2)}, u32[]{:S(2)}) collective-permute-start(f32[264,128]{1,0:T(8,128)S(1)} %pack_a.1.after_ref), channel_id=1, source_target_pairs={{0,4},{1,17},{4,8},{5,21},{8,12},{9,25},{12,0},{13,29},{16,20},{17... | collective-permute-start | bytes 405512 | tf_op jit(solution)/shard_map/ppermute | solution.py:429
  6.6 5.1 %pack_b.5 = (f32[2448,128]{1,0:T(8,128)S(1)}, s32[1]{0:T(128)}) custom-call(s32[1]{0:T(128)} %constant.18.clone.1.round_ref, s32[16,16]{1,0:T(8,128)} %mask_ref.1, f32[1024,1024]{1,0:T(8,128)} %b_hbm.1, f32[264,128]{1,0:T(8,128)S(1)} %pack_a.1.after_ref), custom_call_target="tpu_custom_call" | custom-call | bytes 22140000 | tf_op jit(solution)/shard_map/pack_b/pallas_call | solution.py:173
  11.7 0.0 copy-start.2
  11.7 0.0 collective-permute-done.6
  11.7 0.0 collective-permute-done.5
  11.8 0.1 collective-permute-done.4
  11.9 4.0 %collective-permute-start.9 = (f32[1056,128]{1,0:T(8,128)S(1)}, f32[1056,128]{1,0:T(8,128)S(1)}, u32[]{:S(2)}, u32[]{:S(2)}) collective-permute-start(f32[1056,128]{1,0:T(8,128)S(1)} %constant_dynamic-update-slice_fusion.refs_0_), channel_id=1, source_target_pairs={{0,2},{1,9},{4,6},{5,13},{8,10},{9,1},{12,14},{13,5},{16,18},{17,2... | collective-permute-start | bytes 1622024 | tf_op jit(solution)/shard_map/ppermute | solution.py:432
  15.9 2.8 %collective-permute-start.15 = (f32[2448,128]{1,0:T(8,128)S(1)}, f32[2448,128]{1,0:T(8,128)S(1)}, u32[]{:S(2)}, u32[]{:S(2)}) collective-permute-start(f32[2448,128]{1,0:T(8,128)S(1)} %get-tuple-element.136.refs_3_), channel_id=1, source_target_pairs={{0,96},{32,0},{64,32},{96,64},{1,97},{33,1},{65,33},{97,65},{2,98}... | collective-permute-start | bytes 3760136 | tf_op jit(solution)/shard_map/ppermute | solution.py:443
  18.6 0.7 collective-permute-start.8
  19.3 1.3 %collective-permute-start.7 = (f32[1056,128]{1,0:T(8,128)S(1)}, f32[1056,128]{1,0:T(8,128)S(1)}, u32[]{:S(2)}, u32[]{:S(2)}) collective-permute-start(f32[1056,128]{1,0:T(8,128)S(1)} %constant_dynamic-update-slice_fusion.refs_0_), channel_id=1, source_target_pairs={{0,16},{1,5},{4,20},{5,9},{8,24},{9,13},{12,28},{13,1},{16,2},{17,... | collective-permute-start | bytes 1622024 | tf_op jit(solution)/shard_map/ppermute | solution.py:432
  20.7 2.5 %collective-permute-done.9.refs_3_ = f32[1056,128]{1,0:T(8,128)S(1)} collective-permute-done((f32[1056,128]{1,0:T(8,128)S(1)}, f32[1056,128]{1,0:T(8,128)S(1)}, u32[]{:S(2)}, u32[]{:S(2)}) %collective-permute-start.9) | collective-permute-done | bytes 540704 | tf_op jit(solution)/shard_map/ppermute | solution.py:432
  23.2 0.0 collective-permute-start.12
  23.2 6.8 %collective-permute-done.8.refs_2_ = f32[1056,128]{1,0:T(8,128)S(1)} collective-permute-done((f32[1056,128]{1,0:T(8,128)S(1)}, f32[1056,128]{1,0:T(8,128)S(1)}, u32[]{:S(2)}, u32[]{:S(2)}) %collective-permute-start.8) | collective-permute-done | bytes 540704 | tf_op jit(solution)/shard_map/ppermute | solution.py:432
  30.1 0.5 collective-permute-start.11
  30.6 0.0 collective-permute-start.10
  30.6 2.2 %collective-permute-done.11.refs_5_ = f32[1056,128]{1,0:T(8,128)S(1)} collective-permute-done((f32[1056,128]{1,0:T(8,128)S(1)}, f32[1056,128]{1,0:T(8,128)S(1)}, u32[]{:S(2)}, u32[]{:S(2)}) %collective-permute-start.11) | collective-permute-done | bytes 540704 | tf_op jit(solution)/shard_map/ppermute | solution.py:434
  32.8 0.8 %collective-permute-done.10.refs_4_ = f32[1056,128]{1,0:T(8,128)S(1)} collective-permute-done((f32[1056,128]{1,0:T(8,128)S(1)}, f32[1056,128]{1,0:T(8,128)S(1)}, u32[]{:S(2)}, u32[]{:S(2)}) %collective-permute-start.10) | collective-permute-done | bytes 540704 | tf_op jit(solution)/shard_map/ppermute | solution.py:434
  33.5 7.9 %unpack_a.1 = (bf16[24832,128]{1,0:T(8,128)(2,1)}, s32[1024]{0:T(1024)S(1)}, s32[1]{0:T(128)}) custom-call(f32[1056,128]{1,0:T(8,128)S(1)} %constant_dynamic-update-slice_fusion.refs_0_, f32[1056,128]{1,0:T(8,128)S(1)} %collective-permute-done.7.refs_1_, f32[1056,128]{1,0:T(8,128)S(1)} %collective-permute-done.8.refs_2_, ...), custom_call_target="tpu_custom_call" | custom-call | bytes 22140000 | tf_op jit(solution)/shard_map/unpack_a/pallas_call | solution.py:244
  41.5 2.4 %collective-permute-done.15.refs_5_ = f32[2448,128]{1,0:T(8,128)S(1)} collective-permute-done((f32[2448,128]{1,0:T(8,128)S(1)}, f32[2448,128]{1,0:T(8,128)S(1)}, u32[]{:S(2)}, u32[]{:S(2)}) %collective-permute-start.15) | collective-permute-done | bytes 1253408 | tf_op jit(solution)/shard_map/ppermute | solution.py:443
  43.9 3.4 %collective-permute-done.14.refs_4_ = f32[2448,128]{1,0:T(8,128)S(1)} collective-permute-done((f32[2448,128]{1,0:T(8,128)S(1)}, f32[2448,128]{1,0:T(8,128)S(1)}, u32[]{:S(2)}, u32[]{:S(2)}) %collective-permute-start.14) | collective-permute-done | bytes 1253408 | tf_op jit(solution)/shard_map/ppermute | solution.py:443
  47.3 0.9 %slice.18 = f32[1224,128]{1,0:T(8,128)} slice(f32[2448,128]{1,0:T(8,128)S(1)} %collective-permute-done.14.refs_4_), slice={[0:1224], [0:128]} | slice | bytes 1253376 | tf_op jit(solution)/shard_map/slice | solution.py:447
  48.2 0.9 %slice.19 = f32[1224,128]{1,0:T(8,128)} slice(f32[2448,128]{1,0:T(8,128)S(1)} %collective-permute-done.15.refs_5_), slice={[1224:2448], [0:128]} | slice | bytes 1253376 | tf_op jit(solution)/shard_map/slice | solution.py:447
  49.1 0.3 collective-permute-start.17
  49.4 1.7 %collective-permute-start.16 = (f32[1224,128]{1,0:T(8,128)}, f32[1224,128]{1,0:T(8,128)}, u32[]{:S(2)}, u32[]{:S(2)}) collective-permute-start(f32[1224,128]{1,0:T(8,128)} %slice.18), channel_id=1, source_target_pairs={{0,32},{32,64},{64,96},{96,0},{1,33},{33,65},{65,97},{97,1},{2,34}... | collective-permute-start | bytes 1880072 | tf_op jit(solution)/shard_map/ppermute | solution.py:447
  51.2 1.3 %copy-done.3 = f32[2448,128]{1,0:T(8,128)S(1)} copy-done((f32[2448,128]{1,0:T(8,128)S(1)}, f32[2448,128]{1,0:T(8,128)}, u32[]{:S(2)}) %copy-start.3) | copy-done | bytes 1253400
  52.5 11.3 %product_first.1 = (f32[136,64,128]{2,1,0:T(8,128)S(1)}, s32[1]{0:T(128)}) custom-call(bf16[24832,128]{1,0:T(8,128)(2,1)} %get-tuple-element.224.refs_0_, s32[1024]{0:T(1024)S(1)} %get-tuple-element.225.refs_1_, s32[1]{0:T(128)} %get-tuple-element.138.refs_2_, f32[2448,128]{1,0:T(8,128)S(1)} %copy-done.3, f32[2448,128]{1,0:T(8,128)S(1)} %collective-permute-done.14.refs_4_, ...), custom_call_target="tpu_custom_call" | custom-call | bytes 73800000 | tf_op jit(solution)/shard_map/product_first/pallas_call | solution.py:400
  63.8 0.3 collective-permute-done.16.refs_3_
  64.1 6.6 %product_last.5 = (f32[136,64,128]{2,1,0:T(8,128)S(1)}, f32[1024,1024]{1,0:T(8,128)}, s32[1]{0:T(128)}) custom-call(bf16[24832,128]{1,0:T(8,128)(2,1)S(1)} %copy-done.4, s32[1024]{0:T(1024)S(1)} %get-tuple-element.225.refs_1_, f32[136,64,128]{2,1,0:T(8,128)S(1)} %get-tuple-element.141.refs_2_, ...), custom_call_target="tpu_custom_call", output_to_operand_aliasing={{0}: (2, {})} | custom-call | bytes 29520000 | tf_op jit(solution)/shard_map/product_last/pallas_call | solution.py:400
  72.0 0.2 while.12
  (16 shorter events, 0.1 us)
Async XLA Ops:
  1.2 10.5 %collective-permute-start.6 = (f32[264,128]{1,0:T(8,128)S(1)}, f32[264,128]{1,0:T(8,128)S(1)}, u32[]{:S(2)}, u32[]{:S(2)}) collective-permute-start(f32[264,128]{1,0:T(8,128)S(1)} %pack_a.1.after_ref), channel_id=1, source_target_pairs={{0,8},{1,3},{4,12},{5,7},{8,0},{9,11},{12,4},{13,15},{16,24},{17,1... | collective-permute-start | bytes 405512 | tf_op jit(solution)/shard_map/ppermute | solution.py:429
  4.6 7.2 %collective-permute-start.5 = (f32[264,128]{1,0:T(8,128)S(1)}, f32[264,128]{1,0:T(8,128)S(1)}, u32[]{:S(2)}, u32[]{:S(2)}) collective-permute-start(f32[264,128]{1,0:T(8,128)S(1)} %pack_a.1.after_ref), channel_id=1, source_target_pairs={{0,12},{1,19},{4,0},{5,23},{8,4},{9,27},{12,8},{13,31},{16,28},{17... | collective-permute-start | bytes 405512 | tf_op jit(solution)/shard_map/ppermute | solution.py:429
  5.6 6.2 %collective-permute-start.4 = (f32[264,128]{1,0:T(8,128)S(1)}, f32[264,128]{1,0:T(8,128)S(1)}, u32[]{:S(2)}, u32[]{:S(2)}) collective-permute-start(f32[264,128]{1,0:T(8,128)S(1)} %pack_a.1.after_ref), channel_id=1, source_target_pairs={{0,4},{1,17},{4,8},{5,21},{8,12},{9,25},{12,0},{13,29},{16,20},{17... | collective-permute-start | bytes 405512 | tf_op jit(solution)/shard_map/ppermute | solution.py:429
  11.7 35.6 %copy-start.2 = (f32[2448,128]{1,0:T(8,128)}, f32[2448,128]{1,0:T(8,128)S(1)}, u32[]{:S(2)}) copy-start(f32[2448,128]{1,0:T(8,128)S(1)} %get-tuple-element.136.refs_3_) | copy-start | bytes 3760132
  11.9 11.3 %collective-permute-start.9 = (f32[1056,128]{1,0:T(8,128)S(1)}, f32[1056,128]{1,0:T(8,128)S(1)}, u32[]{:S(2)}, u32[]{:S(2)}) collective-permute-start(f32[1056,128]{1,0:T(8,128)S(1)} %constant_dynamic-update-slice_fusion.refs_0_), channel_id=1, source_target_pairs={{0,2},{1,9},{4,6},{5,13},{8,10},{9,1},{12,14},{13,5},{16,18},{17,2... | collective-permute-start | bytes 1622024 | tf_op jit(solution)/shard_map/ppermute | solution.py:432
  15.9 28.0 %collective-permute-start.15 = (f32[2448,128]{1,0:T(8,128)S(1)}, f32[2448,128]{1,0:T(8,128)S(1)}, u32[]{:S(2)}, u32[]{:S(2)}) collective-permute-start(f32[2448,128]{1,0:T(8,128)S(1)} %get-tuple-element.136.refs_3_), channel_id=1, source_target_pairs={{0,96},{32,0},{64,32},{96,64},{1,97},{33,1},{65,33},{97,65},{2,98}... | collective-permute-start | bytes 3760136 | tf_op jit(solution)/shard_map/ppermute | solution.py:443
  18.6 28.7 %collective-permute-start.14 = (f32[2448,128]{1,0:T(8,128)S(1)}, f32[2448,128]{1,0:T(8,128)S(1)}, u32[]{:S(2)}, u32[]{:S(2)}) collective-permute-start(f32[2448,128]{1,0:T(8,128)S(1)} %get-tuple-element.136.refs_3_), channel_id=1, source_target_pairs={{0,32},{32,64},{64,96},{96,0},{1,33},{33,65},{65,97},{97,1},{2,34}... | collective-permute-start | bytes 3760136 | tf_op jit(solution)/shard_map/ppermute | solution.py:443
  18.6 11.4 %collective-permute-start.8 = (f32[1056,128]{1,0:T(8,128)S(1)}, f32[1056,128]{1,0:T(8,128)S(1)}, u32[]{:S(2)}, u32[]{:S(2)}) collective-permute-start(f32[1056,128]{1,0:T(8,128)S(1)} %constant_dynamic-update-slice_fusion.refs_0_), channel_id=1, source_target_pairs={{0,18},{1,13},{4,22},{5,1},{8,26},{9,5},{12,30},{13,9},{16,0},{17,... | collective-permute-start | bytes 1622024 | tf_op jit(solution)/shard_map/ppermute | solution.py:432
  19.3 10.7 %collective-permute-start.7 = (f32[1056,128]{1,0:T(8,128)S(1)}, f32[1056,128]{1,0:T(8,128)S(1)}, u32[]{:S(2)}, u32[]{:S(2)}) collective-permute-start(f32[1056,128]{1,0:T(8,128)S(1)} %constant_dynamic-update-slice_fusion.refs_0_), channel_id=1, source_target_pairs={{0,16},{1,5},{4,20},{5,9},{8,24},{9,13},{12,28},{13,1},{16,2},{17,... | collective-permute-start | bytes 1622024 | tf_op jit(solution)/shard_map/ppermute | solution.py:432
  23.2 7.4 %collective-permute-start.12 = (f32[1056,128]{1,0:T(8,128)S(1)}, f32[1056,128]{1,0:T(8,128)S(1)}, u32[]{:S(2)}, u32[]{:S(2)}) collective-permute-start(f32[1056,128]{1,0:T(8,128)S(1)} %collective-permute-done.9.refs_3_), channel_id=1, source_target_pairs={{0,1},{1,0},{2,3},{3,2},{4,5},{5,4},{6,7},{7,6},{8,9},{9,8},{10,11... | collective-permute-start | bytes 1622024 | tf_op jit(solution)/shard_map/ppermute | solution.py:434
  30.1 2.7 %collective-permute-start.13 = (f32[1056,128]{1,0:T(8,128)S(1)}, f32[1056,128]{1,0:T(8,128)S(1)}, u32[]{:S(2)}, u32[]{:S(2)}) collective-permute-start(f32[1056,128]{1,0:T(8,128)S(1)} %constant_dynamic-update-slice_fusion.refs_0_), channel_id=1, source_target_pairs={{0,1},{1,0},{2,3},{3,2},{4,5},{5,4},{6,7},{7,6},{8,9},{9,8},{10,11... | collective-permute-start | bytes 1622024 | tf_op jit(solution)/shard_map/ppermute | solution.py:434
  30.1 2.7 %collective-permute-start.11 = (f32[1056,128]{1,0:T(8,128)S(1)}, f32[1056,128]{1,0:T(8,128)S(1)}, u32[]{:S(2)}, u32[]{:S(2)}) collective-permute-start(f32[1056,128]{1,0:T(8,128)S(1)} %collective-permute-done.8.refs_2_), channel_id=1, source_target_pairs={{0,1},{1,0},{2,3},{3,2},{4,5},{5,4},{6,7},{7,6},{8,9},{9,8},{10,11... | collective-permute-start | bytes 1622024 | tf_op jit(solution)/shard_map/ppermute | solution.py:434
  30.6 3.0 %collective-permute-start.10 = (f32[1056,128]{1,0:T(8,128)S(1)}, f32[1056,128]{1,0:T(8,128)S(1)}, u32[]{:S(2)}, u32[]{:S(2)}) collective-permute-start(f32[1056,128]{1,0:T(8,128)S(1)} %collective-permute-done.7.refs_1_), channel_id=1, source_target_pairs={{0,1},{1,0},{2,3},{3,2},{4,5},{5,4},{6,7},{7,6},{8,9},{9,8},{10,11... | collective-permute-start | bytes 1622024 | tf_op jit(solution)/shard_map/ppermute | solution.py:434
  49.1 14.7 %collective-permute-start.17 = (f32[1224,128]{1,0:T(8,128)}, f32[1224,128]{1,0:T(8,128)S(1)}, u32[]{:S(2)}, u32[]{:S(2)}) collective-permute-start(f32[1224,128]{1,0:T(8,128)} %slice.19), channel_id=1, source_target_pairs={{0,96},{32,0},{64,32},{96,64},{1,97},{33,1},{65,33},{97,65},{2,98}... | collective-permute-start | bytes 1880072 | tf_op jit(solution)/shard_map/ppermute | solution.py:447
  49.4 14.7 %collective-permute-start.16 = (f32[1224,128]{1,0:T(8,128)}, f32[1224,128]{1,0:T(8,128)}, u32[]{:S(2)}, u32[]{:S(2)}) collective-permute-start(f32[1224,128]{1,0:T(8,128)} %slice.18), channel_id=1, source_target_pairs={{0,32},{32,64},{64,96},{96,0},{1,33},{33,65},{65,97},{97,1},{2,34}... | collective-permute-start | bytes 1880072 | tf_op jit(solution)/shard_map/ppermute | solution.py:447
  51.2 1.3 %copy-start.3 = (f32[2448,128]{1,0:T(8,128)S(1)}, f32[2448,128]{1,0:T(8,128)}, u32[]{:S(2)}) copy-start(f32[2448,128]{1,0:T(8,128)} %copy-done.2) | copy-start | bytes 3760132
  52.5 11.6 %copy-start.4 = (bf16[24832,128]{1,0:T(8,128)(2,1)S(1)}, bf16[24832,128]{1,0:T(8,128)(2,1)}, u32[]{:S(2)}) copy-start(bf16[24832,128]{1,0:T(8,128)(2,1)} %get-tuple-element.224.refs_0_) | copy-start | bytes 19070980
  64.1 7.9 %copy-start.5 = (s32[16,16]{1,0:T(8,128)S(1)}, s32[16,16]{1,0:T(8,128)}, u32[]{:S(2)}) copy-start(s32[16,16]{1,0:T(8,128)} %mask_ref.1) | copy-start | bytes 3076

commit v4 on v3

--- a/solution.py
+++ b/solution.py
@@ -16,7 +16,7 @@
 MESSAGES = 8
 H_K, H_J0, H_J1, H_L0, H_R0, H_L1, H_R1, H_COUNT = range(8)
 E_STRIDE = 44
-UNROLL = 6
+UNROLL = 8
 UNPACK = 4
 A_SHARDS = 32
 A_PER_GROUP = 4

time: 73.3 us -> 73.2 us (level)
  Pallas kernels: 32.1 us -> 30.8 us
  waiting for transfers between devices: 18.6 us -> 19.5 us
    pallas_call x2, Pallas kernels: 17.9 us -> 16.5 us  [product(): pl.pallas_call(kernel, in_specs=in_specs, out_specs=out_specs, out_shape=...]
    ppermute x1, waiting for transfers between devices: 0.26 us -> 1.16 us  [far_b(): lax.ppermute(above[:B_ROWS], 'row', UP)]
  transfers between devices with their start and end apart: 14 -> 14, of which waited for: 8 -> 8; matrix products, arithmetic and copies ran while one was open for 0% -> 0% of each run, Pallas kernels for 34% -> 33%
where the time goes in v4:
time: 73.2 us; the launch traced here: 71.9 us
  Pallas kernels  30.8 us (42%)
  waiting for transfers between devices  19.5 us (27%)
  starting transfers between devices  16.7 us (23%)
  local copies, waits for them, and re-layouts  3.17 us (4%)
  between operations  1.6 us (2%)
    pallas_call x2, Pallas kernels, product(): pl.pallas_call(kernel, in_specs=in_specs, out_specs=out_specs, out_shape=...  16.5 us
    ppermute x3, waiting for transfers between devices, gather_a(): lax.ppermute(group, AXES, _turn(s, True))  9.39 us
    pallas_call x1, Pallas kernels, unpack_a(): pl.pallas_call(unpack_a_kernel, in_specs=[vmem] * len(a_parts) + [smem],...  7.91 us
    ppermute x3, starting transfers between devices, gather_a(): lax.ppermute(group, AXES, _turn(s, True))  5.98 us
    ppermute x2, waiting for transfers between devices, near_b(): return (lax.ppermute(p, 'row', UP), lax.ppermute(p, 'row', DOWN))  5.86 us
    ppermute x3, starting transfers between devices, gather_a(): lax.ppermute(packed, AXES, _turn(s, False))  5.38 us
    pallas_call x1, Pallas kernels, pack_b(): pl.pallas_call(pack_b_kernel, in_specs=[smem, smem, pl.BlockSpec(memory_s...  5.13 us
    ppermute x4, waiting for transfers between devices, gather_a(): lax.ppermute(x, 'core', [(0, 1), (1, 0)])  2.96 us
  transfers between devices with their start and end apart: 14, of which 8 were waited for; matrix products, arithmetic and copies ran while one was open for 0% of the time, Pallas kernels for 33%

profile of v4, /device:TPU:0, one launch (start us, length us, event | category | flops | bytes accessed | tf_op | source)
XLA Modules:
  0.0 71.9 jit_solution(10154792676049801749)
XLA Ops:
  0.0 1.2 %pack_a.1.after_ref = f32[264,128]{1,0:T(8,128)S(1)} custom-call(s32[2,16]{1,0:T(2,128)} %bitcast.22, f32[1024,128]{1,0:T(8,128)} %a_ref.1), custom_call_target="tpu_custom_call" | custom-call | bytes 7380000 | tf_op jit(solution)/shard_map/pack_a/pallas_call | solution.py:75
  1.2 3.4 %collective-permute-start.6 = (f32[264,128]{1,0:T(8,128)S(1)}, f32[264,128]{1,0:T(8,128)S(1)}, u32[]{:S(2)}, u32[]{:S(2)}) collective-permute-start(f32[264,128]{1,0:T(8,128)S(1)} %pack_a.1.after_ref), channel_id=1, source_target_pairs={{0,8},{1,3},{4,12},{5,7},{8,0},{9,11},{12,4},{13,15},{16,24},{17,1... | collective-permute-start | bytes 405512 | tf_op jit(solution)/shard_map/ppermute | solution.py:429
  4.6 1.1 %collective-permute-start.5 = (f32[264,128]{1,0:T(8,128)S(1)}, f32[264,128]{1,0:T(8,128)S(1)}, u32[]{:S(2)}, u32[]{:S(2)}) collective-permute-start(f32[264,128]{1,0:T(8,128)S(1)} %pack_a.1.after_ref), channel_id=1, source_target_pairs={{0,12},{1,19},{4,0},{5,23},{8,4},{9,27},{12,8},{13,31},{16,28},{17... | collective-permute-start | bytes 405512 | tf_op jit(solution)/shard_map/ppermute | solution.py:429
  5.6 1.0 %collective-permute-start.4 = (f32[264,128]{1,0:T(8,128)S(1)}, f32[264,128]{1,0:T(8,128)S(1)}, u32[]{:S(2)}, u32[]{:S(2)}) collective-permute-start(f32[264,128]{1,0:T(8,128)S(1)} %pack_a.1.after_ref), channel_id=1, source_target_pairs={{0,4},{1,17},{4,8},{5,21},{8,12},{9,25},{12,0},{13,29},{16,20},{17... | collective-permute-start | bytes 405512 | tf_op jit(solution)/shard_map/ppermute | solution.py:429
  6.6 5.1 %pack_b.5 = (f32[2448,128]{1,0:T(8,128)S(1)}, s32[1]{0:T(128)}) custom-call(s32[1]{0:T(128)} %constant.18.clone.1.round_ref, s32[16,16]{1,0:T(8,128)} %mask_ref.1, f32[1024,1024]{1,0:T(8,128)} %b_hbm.1, f32[264,128]{1,0:T(8,128)S(1)} %pack_a.1.after_ref), custom_call_target="tpu_custom_call" | custom-call | bytes 22140000 | tf_op jit(solution)/shard_map/pack_b/pallas_call | solution.py:173
  11.7 0.0 copy-start.2
  11.7 0.0 collective-permute-done.6
  11.7 0.0 collective-permute-done.5
  11.8 0.1 collective-permute-done.4
  11.9 4.0 %collective-permute-start.9 = (f32[1056,128]{1,0:T(8,128)S(1)}, f32[1056,128]{1,0:T(8,128)S(1)}, u32[]{:S(2)}, u32[]{:S(2)}) collective-permute-start(f32[1056,128]{1,0:T(8,128)S(1)} %constant_dynamic-update-slice_fusion.refs_0_), channel_id=1, source_target_pairs={{0,2},{1,9},{4,6},{5,13},{8,10},{9,1},{12,14},{13,5},{16,18},{17,2... | collective-permute-start | bytes 1622024 | tf_op jit(solution)/shard_map/ppermute | solution.py:432
  15.9 2.8 %collective-permute-start.15 = (f32[2448,128]{1,0:T(8,128)S(1)}, f32[2448,128]{1,0:T(8,128)S(1)}, u32[]{:S(2)}, u32[]{:S(2)}) collective-permute-start(f32[2448,128]{1,0:T(8,128)S(1)} %get-tuple-element.136.refs_3_), channel_id=1, source_target_pairs={{0,96},{32,0},{64,32},{96,64},{1,97},{33,1},{65,33},{97,65},{2,98}... | collective-permute-start | bytes 3760136 | tf_op jit(solution)/shard_map/ppermute | solution.py:443
  18.6 0.7 collective-permute-start.8
  19.3 1.3 %collective-permute-start.7 = (f32[1056,128]{1,0:T(8,128)S(1)}, f32[1056,128]{1,0:T(8,128)S(1)}, u32[]{:S(2)}, u32[]{:S(2)}) collective-permute-start(f32[1056,128]{1,0:T(8,128)S(1)} %constant_dynamic-update-slice_fusion.refs_0_), channel_id=1, source_target_pairs={{0,16},{1,5},{4,20},{5,9},{8,24},{9,13},{12,28},{13,1},{16,2},{17,... | collective-permute-start | bytes 1622024 | tf_op jit(solution)/shard_map/ppermute | solution.py:432
  20.7 2.5 %collective-permute-done.9.refs_3_ = f32[1056,128]{1,0:T(8,128)S(1)} collective-permute-done((f32[1056,128]{1,0:T(8,128)S(1)}, f32[1056,128]{1,0:T(8,128)S(1)}, u32[]{:S(2)}, u32[]{:S(2)}) %collective-permute-start.9) | collective-permute-done | bytes 540704 | tf_op jit(solution)/shard_map/ppermute | solution.py:432
  23.2 6.8 %collective-permute-done.8.refs_2_ = f32[1056,128]{1,0:T(8,128)S(1)} collective-permute-done((f32[1056,128]{1,0:T(8,128)S(1)}, f32[1056,128]{1,0:T(8,128)S(1)}, u32[]{:S(2)}, u32[]{:S(2)}) %collective-permute-start.8) | collective-permute-done | bytes 540704 | tf_op jit(solution)/shard_map/ppermute | solution.py:432
  30.1 0.5 collective-permute-start.11
  30.6 0.0 collective-permute-start.10
  30.6 2.2 %collective-permute-done.11.refs_5_ = f32[1056,128]{1,0:T(8,128)S(1)} collective-permute-done((f32[1056,128]{1,0:T(8,128)S(1)}, f32[1056,128]{1,0:T(8,128)S(1)}, u32[]{:S(2)}, u32[]{:S(2)}) %collective-permute-start.11) | collective-permute-done | bytes 540704 | tf_op jit(solution)/shard_map/ppermute | solution.py:434
  32.8 0.8 %collective-permute-done.10.refs_4_ = f32[1056,128]{1,0:T(8,128)S(1)} collective-permute-done((f32[1056,128]{1,0:T(8,128)S(1)}, f32[1056,128]{1,0:T(8,128)S(1)}, u32[]{:S(2)}, u32[]{:S(2)}) %collective-permute-start.10) | collective-permute-done | bytes 540704 | tf_op jit(solution)/shard_map/ppermute | solution.py:434
  33.5 7.9 %unpack_a.1 = (bf16[24832,128]{1,0:T(8,128)(2,1)}, s32[1024]{0:T(1024)S(1)}, s32[1]{0:T(128)}) custom-call(f32[1056,128]{1,0:T(8,128)S(1)} %constant_dynamic-update-slice_fusion.refs_0_, f32[1056,128]{1,0:T(8,128)S(1)} %collective-permute-done.7.refs_1_, f32[1056,128]{1,0:T(8,128)S(1)} %collective-permute-done.8.refs_2_, ...), custom_call_target="tpu_custom_call" | custom-call | bytes 22140000 | tf_op jit(solution)/shard_map/unpack_a/pallas_call | solution.py:244
  41.5 2.4 %collective-permute-done.15.refs_5_ = f32[2448,128]{1,0:T(8,128)S(1)} collective-permute-done((f32[2448,128]{1,0:T(8,128)S(1)}, f32[2448,128]{1,0:T(8,128)S(1)}, u32[]{:S(2)}, u32[]{:S(2)}) %collective-permute-start.15) | collective-permute-done | bytes 1253408 | tf_op jit(solution)/shard_map/ppermute | solution.py:443
  43.9 3.4 %collective-permute-done.14.refs_4_ = f32[2448,128]{1,0:T(8,128)S(1)} collective-permute-done((f32[2448,128]{1,0:T(8,128)S(1)}, f32[2448,128]{1,0:T(8,128)S(1)}, u32[]{:S(2)}, u32[]{:S(2)}) %collective-permute-start.14) | collective-permute-done | bytes 1253408 | tf_op jit(solution)/shard_map/ppermute | solution.py:443
  47.3 0.9 %slice.18 = f32[1224,128]{1,0:T(8,128)} slice(f32[2448,128]{1,0:T(8,128)S(1)} %collective-permute-done.14.refs_4_), slice={[0:1224], [0:128]} | slice | bytes 1253376 | tf_op jit(solution)/shard_map/slice | solution.py:447
  48.2 0.9 %slice.19 = f32[1224,128]{1,0:T(8,128)} slice(f32[2448,128]{1,0:T(8,128)S(1)} %collective-permute-done.15.refs_5_), slice={[1224:2448], [0:128]} | slice | bytes 1253376 | tf_op jit(solution)/shard_map/slice | solution.py:447
  49.1 0.3 collective-permute-start.17
  49.4 1.7 %collective-permute-start.16 = (f32[1224,128]{1,0:T(8,128)}, f32[1224,128]{1,0:T(8,128)}, u32[]{:S(2)}, u32[]{:S(2)}) collective-permute-start(f32[1224,128]{1,0:T(8,128)} %slice.18), channel_id=1, source_target_pairs={{0,32},{32,64},{64,96},{96,0},{1,33},{33,65},{65,97},{97,1},{2,34}... | collective-permute-start | bytes 1880072 | tf_op jit(solution)/shard_map/ppermute | solution.py:447
  51.2 1.3 %copy-done.3 = f32[2448,128]{1,0:T(8,128)S(1)} copy-done((f32[2448,128]{1,0:T(8,128)S(1)}, f32[2448,128]{1,0:T(8,128)}, u32[]{:S(2)}) %copy-start.3) | copy-done | bytes 1253400
  52.5 10.4 %product_first.1 = (f32[136,64,128]{2,1,0:T(8,128)S(1)}, s32[1]{0:T(128)}) custom-call(bf16[24832,128]{1,0:T(8,128)(2,1)} %get-tuple-element.224.refs_0_, s32[1024]{0:T(1024)S(1)} %get-tuple-element.225.refs_1_, s32[1]{0:T(128)} %get-tuple-element.138.refs_2_, f32[2448,128]{1,0:T(8,128)S(1)} %copy-done.3, f32[2448,128]{1,0:T(8,128)S(1)} %collective-permute-done.14.refs_4_, ...), custom_call_target="tpu_custom_call" | custom-call | bytes 73800000 | tf_op jit(solution)/shard_map/product_first/pallas_call | solution.py:400
  62.9 0.0 collective-permute-done.17.refs_4_
  62.9 1.2 %collective-permute-done.16.refs_3_ = f32[1224,128]{1,0:T(8,128)} collective-permute-done((f32[1224,128]{1,0:T(8,128)}, f32[1224,128]{1,0:T(8,128)}, u32[]{:S(2)}, u32[]{:S(2)}) %collective-permute-start.16) | collective-permute-done | bytes 626720 | tf_op jit(solution)/shard_map/ppermute | solution.py:447
  64.1 6.1 %product_last.5 = (f32[136,64,128]{2,1,0:T(8,128)S(1)}, f32[1024,1024]{1,0:T(8,128)}, s32[1]{0:T(128)}) custom-call(bf16[24832,128]{1,0:T(8,128)(2,1)S(1)} %copy-done.4, s32[1024]{0:T(1024)S(1)} %get-tuple-element.225.refs_1_, f32[136,64,128]{2,1,0:T(8,128)S(1)} %get-tuple-element.141.refs_2_, ...), custom_call_target="tpu_custom_call", output_to_operand_aliasing={{0}: (2, {})} | custom-call | bytes 29520000 | tf_op jit(solution)/shard_map/product_last/pallas_call | solution.py:400
  71.5 0.2 while.12
  (16 shorter events, 0.1 us)
Async XLA Ops:
  1.2 10.5 %collective-permute-start.6 = (f32[264,128]{1,0:T(8,128)S(1)}, f32[264,128]{1,0:T(8,128)S(1)}, u32[]{:S(2)}, u32[]{:S(2)}) collective-permute-start(f32[264,128]{1,0:T(8,128)S(1)} %pack_a.1.after_ref), channel_id=1, source_target_pairs={{0,8},{1,3},{4,12},{5,7},{8,0},{9,11},{12,4},{13,15},{16,24},{17,1... | collective-permute-start | bytes 405512 | tf_op jit(solution)/shard_map/ppermute | solution.py:429
  4.6 7.2 %collective-permute-start.5 = (f32[264,128]{1,0:T(8,128)S(1)}, f32[264,128]{1,0:T(8,128)S(1)}, u32[]{:S(2)}, u32[]{:S(2)}) collective-permute-start(f32[264,128]{1,0:T(8,128)S(1)} %pack_a.1.after_ref), channel_id=1, source_target_pairs={{0,12},{1,19},{4,0},{5,23},{8,4},{9,27},{12,8},{13,31},{16,28},{17... | collective-permute-start | bytes 405512 | tf_op jit(solution)/shard_map/ppermute | solution.py:429
  5.6 6.2 %collective-permute-start.4 = (f32[264,128]{1,0:T(8,128)S(1)}, f32[264,128]{1,0:T(8,128)S(1)}, u32[]{:S(2)}, u32[]{:S(2)}) collective-permute-start(f32[264,128]{1,0:T(8,128)S(1)} %pack_a.1.after_ref), channel_id=1, source_target_pairs={{0,4},{1,17},{4,8},{5,21},{8,12},{9,25},{12,0},{13,29},{16,20},{17... | collective-permute-start | bytes 405512 | tf_op jit(solution)/shard_map/ppermute | solution.py:429
  11.7 35.6 %copy-start.2 = (f32[2448,128]{1,0:T(8,128)}, f32[2448,128]{1,0:T(8,128)S(1)}, u32[]{:S(2)}) copy-start(f32[2448,128]{1,0:T(8,128)S(1)} %get-tuple-element.136.refs_3_) | copy-start | bytes 3760132
  11.9 11.3 %collective-permute-start.9 = (f32[1056,128]{1,0:T(8,128)S(1)}, f32[1056,128]{1,0:T(8,128)S(1)}, u32[]{:S(2)}, u32[]{:S(2)}) collective-permute-start(f32[1056,128]{1,0:T(8,128)S(1)} %constant_dynamic-update-slice_fusion.refs_0_), channel_id=1, source_target_pairs={{0,2},{1,9},{4,6},{5,13},{8,10},{9,1},{12,14},{13,5},{16,18},{17,2... | collective-permute-start | bytes 1622024 | tf_op jit(solution)/shard_map/ppermute | solution.py:432
  15.9 28.0 %collective-permute-start.15 = (f32[2448,128]{1,0:T(8,128)S(1)}, f32[2448,128]{1,0:T(8,128)S(1)}, u32[]{:S(2)}, u32[]{:S(2)}) collective-permute-start(f32[2448,128]{1,0:T(8,128)S(1)} %get-tuple-element.136.refs_3_), channel_id=1, source_target_pairs={{0,96},{32,0},{64,32},{96,64},{1,97},{33,1},{65,33},{97,65},{2,98}... | collective-permute-start | bytes 3760136 | tf_op jit(solution)/shard_map/ppermute | solution.py:443
  18.6 28.7 %collective-permute-start.14 = (f32[2448,128]{1,0:T(8,128)S(1)}, f32[2448,128]{1,0:T(8,128)S(1)}, u32[]{:S(2)}, u32[]{:S(2)}) collective-permute-start(f32[2448,128]{1,0:T(8,128)S(1)} %get-tuple-element.136.refs_3_), channel_id=1, source_target_pairs={{0,32},{32,64},{64,96},{96,0},{1,33},{33,65},{65,97},{97,1},{2,34}... | collective-permute-start | bytes 3760136 | tf_op jit(solution)/shard_map/ppermute | solution.py:443
  18.6 11.4 %collective-permute-start.8 = (f32[1056,128]{1,0:T(8,128)S(1)}, f32[1056,128]{1,0:T(8,128)S(1)}, u32[]{:S(2)}, u32[]{:S(2)}) collective-permute-start(f32[1056,128]{1,0:T(8,128)S(1)} %constant_dynamic-update-slice_fusion.refs_0_), channel_id=1, source_target_pairs={{0,18},{1,13},{4,22},{5,1},{8,26},{9,5},{12,30},{13,9},{16,0},{17,... | collective-permute-start | bytes 1622024 | tf_op jit(solution)/shard_map/ppermute | solution.py:432
  19.3 10.7 %collective-permute-start.7 = (f32[1056,128]{1,0:T(8,128)S(1)}, f32[1056,128]{1,0:T(8,128)S(1)}, u32[]{:S(2)}, u32[]{:S(2)}) collective-permute-start(f32[1056,128]{1,0:T(8,128)S(1)} %constant_dynamic-update-slice_fusion.refs_0_), channel_id=1, source_target_pairs={{0,16},{1,5},{4,20},{5,9},{8,24},{9,13},{12,28},{13,1},{16,2},{17,... | collective-permute-start | bytes 1622024 | tf_op jit(solution)/shard_map/ppermute | solution.py:432
  23.2 7.4 %collective-permute-start.12 = (f32[1056,128]{1,0:T(8,128)S(1)}, f32[1056,128]{1,0:T(8,128)S(1)}, u32[]{:S(2)}, u32[]{:S(2)}) collective-permute-start(f32[1056,128]{1,0:T(8,128)S(1)} %collective-permute-done.9.refs_3_), channel_id=1, source_target_pairs={{0,1},{1,0},{2,3},{3,2},{4,5},{5,4},{6,7},{7,6},{8,9},{9,8},{10,11... | collective-permute-start | bytes 1622024 | tf_op jit(solution)/shard_map/ppermute | solution.py:434
  30.1 2.7 %collective-permute-start.13 = (f32[1056,128]{1,0:T(8,128)S(1)}, f32[1056,128]{1,0:T(8,128)S(1)}, u32[]{:S(2)}, u32[]{:S(2)}) collective-permute-start(f32[1056,128]{1,0:T(8,128)S(1)} %constant_dynamic-update-slice_fusion.refs_0_), channel_id=1, source_target_pairs={{0,1},{1,0},{2,3},{3,2},{4,5},{5,4},{6,7},{7,6},{8,9},{9,8},{10,11... | collective-permute-start | bytes 1622024 | tf_op jit(solution)/shard_map/ppermute | solution.py:434
  30.1 2.7 %collective-permute-start.11 = (f32[1056,128]{1,0:T(8,128)S(1)}, f32[1056,128]{1,0:T(8,128)S(1)}, u32[]{:S(2)}, u32[]{:S(2)}) collective-permute-start(f32[1056,128]{1,0:T(8,128)S(1)} %collective-permute-done.8.refs_2_), channel_id=1, source_target_pairs={{0,1},{1,0},{2,3},{3,2},{4,5},{5,4},{6,7},{7,6},{8,9},{9,8},{10,11... | collective-permute-start | bytes 1622024 | tf_op jit(solution)/shard_map/ppermute | solution.py:434
  30.6 3.0 %collective-permute-start.10 = (f32[1056,128]{1,0:T(8,128)S(1)}, f32[1056,128]{1,0:T(8,128)S(1)}, u32[]{:S(2)}, u32[]{:S(2)}) collective-permute-start(f32[1056,128]{1,0:T(8,128)S(1)} %collective-permute-done.7.refs_1_), channel_id=1, source_target_pairs={{0,1},{1,0},{2,3},{3,2},{4,5},{5,4},{6,7},{7,6},{8,9},{9,8},{10,11... | collective-permute-start | bytes 1622024 | tf_op jit(solution)/shard_map/ppermute | solution.py:434
  49.1 13.8 %collective-permute-start.17 = (f32[1224,128]{1,0:T(8,128)}, f32[1224,128]{1,0:T(8,128)S(1)}, u32[]{:S(2)}, u32[]{:S(2)}) collective-permute-start(f32[1224,128]{1,0:T(8,128)} %slice.19), channel_id=1, source_target_pairs={{0,96},{32,0},{64,32},{96,64},{1,97},{33,1},{65,33},{97,65},{2,98}... | collective-permute-start | bytes 1880072 | tf_op jit(solution)/shard_map/ppermute | solution.py:447
  49.4 14.7 %collective-permute-start.16 = (f32[1224,128]{1,0:T(8,128)}, f32[1224,128]{1,0:T(8,128)}, u32[]{:S(2)}, u32[]{:S(2)}) collective-permute-start(f32[1224,128]{1,0:T(8,128)} %slice.18), channel_id=1, source_target_pairs={{0,32},{32,64},{64,96},{96,0},{1,33},{33,65},{65,97},{97,1},{2,34}... | collective-permute-start | bytes 1880072 | tf_op jit(solution)/shard_map/ppermute | solution.py:447
  51.2 1.3 %copy-start.3 = (f32[2448,128]{1,0:T(8,128)S(1)}, f32[2448,128]{1,0:T(8,128)}, u32[]{:S(2)}) copy-start(f32[2448,128]{1,0:T(8,128)} %copy-done.2) | copy-start | bytes 3760132
  52.5 11.6 %copy-start.4 = (bf16[24832,128]{1,0:T(8,128)(2,1)S(1)}, bf16[24832,128]{1,0:T(8,128)(2,1)}, u32[]{:S(2)}) copy-start(bf16[24832,128]{1,0:T(8,128)(2,1)} %get-tuple-element.224.refs_0_) | copy-start | bytes 19070980
  64.1 7.4 %copy-start.5 = (s32[16,16]{1,0:T(8,128)S(1)}, s32[16,16]{1,0:T(8,128)}, u32[]{:S(2)}) copy-start(s32[16,16]{1,0:T(8,128)} %mask_ref.1) | copy-start | bytes 3076
